TPU v7x, 128 devices: a whole 4x4x4 slice. The times are simulated.
128 devices in a mesh: ep: 8 (over z, core), dp: 16 (over y, x).
Axes of the slice: x: 4, y: 4, z: 4, core: 2. Of those that a mesh axis runs over, the one named last changes fastest.
Arguments:
- tokens: bfloat16 [32768, 1024], P(('ep', 'dp')), may hold values from -6 to 6
- lengths: int32 [8, 2], P('ep'), may hold values from 1 to 3072, 4096 in all within a row
- adapter_ids: int32 [8, 2], replicated, may hold values from 0 to 63
- expert_ids: int32 [32768, 8], P(('ep', 'dp')), may hold values from 0 to 31, all different within a row; in each aligned block of 256 rows (0 to 255, 256 to 511, ...) at most 96 rows name the same one
- attn_gain: bfloat16 [1024], replicated, may hold values from 0.5 to 1.5
- w_qkv: bfloat16 [1024, 2048], replicated, may hold values from -3 to 3
- w_out: bfloat16 [1024, 1024], replicated, may hold values from -0.1875 to 0.1875
- moe_gain: bfloat16 [1024], replicated, may hold values from 0.5 to 1.5
- w_router: bfloat16 [1024, 32], replicated, may hold values from -12 to 12
- w_gate_up: bfloat16 [32, 1024, 1024], P('ep'), may hold values from -0.1875 to 0.1875
- w_down: bfloat16 [32, 512, 1024], P('ep'), may hold values from -0.25 to 0.25
- adapter_in: bfloat16 [64, 1024, 64], P('dp'), may hold values from -0.1875 to 0.1875
- adapter_out: bfloat16 [64, 16, 4096], P('dp'), may hold values from -0.75 to 0.75
- adapter_expert: bfloat16 [64, 48, 512], P('dp'), may hold values from -0.75 to 0.75
Outputs:
- layer_out: bfloat16 [32768, 1024], P(('ep', 'dp'))
Inputs may be any that keep to these rules, and one draw needn't show every extreme that they name: `lengths`: each row sums to 4096. `expert_ids`: each row names 8 different experts; among the 256 rows of one device no expert is named more than 96 times.
All inputs are finite; a program needn't handle non-finite values.
Results may differ from a plain program's by a relative error of at most 0.02.
The roundings to bfloat16 on the way count: a program that leaves them out, or rounds other values in their place, can miss the bound.
Values may be sent and summed in bfloat16 or wider, within the bound.
A program may use at most 256 MiB of HBM per device.

v0:
```python
import math

import jax
import jax.numpy as jnp
from jax import lax
from jax.sharding import PartitionSpec as P

HEADS = 16
KV_HEADS = 8
HEAD = 64
CAP = 96


EPS = 1e-06
THETA = 10000.0
NEG_BIG = -1e30


def rms_norm(values_in, gain_vec):
    floats = values_in.astype(jnp.float32)
    meansq = jnp.mean(floats * floats, axis=-1, keepdims=True)
    return (floats * lax.rsqrt(meansq + EPS) * gain_vec.astype(jnp.float32)).astype(jnp.bfloat16)


def rotate(vectors, position):
    half_dim = vectors.shape[-1] // 2
    frequency = THETA ** (-jnp.arange(half_dim, dtype=jnp.float32) / half_dim)
    angles = position.astype(jnp.float32)[:, None] * frequency[None, :]
    cosine = jnp.cos(angles)[:, None, :]
    sine_val = jnp.sin(angles)[:, None, :]
    first_half = vectors[..., :half_dim]
    second_half = vectors[..., half_dim:]
    return jnp.concatenate(
        [
            first_half * cosine - second_half * sine_val,
            second_half * cosine + first_half * sine_val,
        ],
        axis=-1,
    )


def request_layout(lengths_row, first_pos, row_count):
    position = first_pos + jnp.arange(row_count, dtype=jnp.int32)
    req_ends = jnp.cumsum(lengths_row)
    starts = req_ends - lengths_row
    request = jnp.sum((position[:, None] >= req_ends[None, :]).astype(jnp.int32), axis=1)
    slot_hot = request[:, None] == jnp.arange(lengths_row.shape[0], dtype=jnp.int32)[None, :]
    req_start = jnp.sum(jnp.where(slot_hot, starts[None, :], 0), axis=1)
    return (position, req_start, slot_hot)


def low_rank(inputs, a_sel, slot_hot):
    count_r = a_sel.shape[2]
    a_cat = jnp.transpose(a_sel, (1, 0, 2)).reshape(inputs.shape[1], -1)
    coeffs = jnp.dot(inputs, a_cat, preferred_element_type=jnp.float32)
    keep_mask = jnp.repeat(slot_hot, count_r, axis=1)
    return jnp.where(keep_mask, coeffs, 0.0).astype(jnp.bfloat16)


def earlier_counts(flat_ids, n_experts):
    expert_hot = (flat_ids[:, None] == jnp.arange(n_experts, dtype=jnp.int32)[None, :]).astype(
        jnp.int32
    )
    return jnp.sum((jnp.cumsum(expert_hot, axis=0) - expert_hot) * expert_hot, axis=1)


def per_device(
    tokens,
    lengths,
    adapter_ids,
    expert_ids,
    attn_gain,
    w_qkv,
    w_out,
    moe_gain,
    w_router,
    w_gate_up,
    w_down,
    adapter_in,
    adapter_out,
    adapter_expert,
):
    n_ep = lax.axis_size("ep")
    group_idx = lax.axis_index("ep")
    row_idx = lax.axis_index("dp")
    tok_count = tokens.shape[0]
    model_width = tokens.shape[1]
    rank_r = adapter_in.shape[2] // 4
    q_width = HEADS * HEAD
    kv_width = KV_HEADS * HEAD
    qkv_width = q_width + 2 * kv_width
    group_ratio = HEADS // KV_HEADS
    ff_width = w_down.shape[1]
    exp_local = w_gate_up.shape[0]
    n_requests = lengths.shape[1]
    top_count = expert_ids.shape[1]
    position, req_start, slot_hot = request_layout(lengths[0], row_idx * tok_count, tok_count)
    group_ids = lax.dynamic_index_in_dim(adapter_ids, group_idx, 0, keepdims=False)
    all_in, all_out, all_expert = (
        lax.all_gather(adapter_in, "dp", axis=0, tiled=True),
        lax.all_gather(adapter_out, "dp", axis=0, tiled=True),
        lax.all_gather(adapter_expert, "dp", axis=0, tiled=True),
    )
    sel_in = jnp.take(all_in, group_ids, axis=0)
    sel_out = jnp.take(all_out, group_ids, axis=0)
    normed = rms_norm(tokens, attn_gain)
    z_qkv = low_rank(normed, sel_in[:, :, 0:rank_r], slot_hot)
    projected = jnp.dot(normed, w_qkv, preferred_element_type=jnp.float32)
    projected = projected + jnp.dot(
        z_qkv, sel_out[:, :, 0:qkv_width].reshape(-1, qkv_width), preferred_element_type=jnp.float32
    )
    rel_pos = position - req_start
    queries = rotate(projected[:, :q_width].reshape(tok_count, HEADS, HEAD), rel_pos).astype(
        jnp.bfloat16
    )
    keys_rot = rotate(
        projected[:, q_width : q_width + kv_width].reshape(tok_count, KV_HEADS, HEAD), rel_pos
    ).astype(jnp.bfloat16)
    keys_rot = keys_rot.reshape(tok_count, kv_width)
    values_v = projected[:, q_width + kv_width :].astype(jnp.bfloat16)
    query_grp = queries.reshape(tok_count, KV_HEADS, group_ratio, HEAD)
    score_scale = 1.0 / math.sqrt(HEAD)
    last_pos = position[tok_count - 1]
    first_start = req_start[0]
    init_state = (
        jnp.full((tok_count, KV_HEADS, group_ratio), NEG_BIG, jnp.float32),
        jnp.zeros((tok_count, KV_HEADS, group_ratio), jnp.float32),
        jnp.zeros((tok_count, KV_HEADS, group_ratio, HEAD), jnp.float32),
    )
    first_row = jnp.int32(0)
    keys_in = lax.all_gather(keys_rot, "dp", axis=0, tiled=True)
    vals_in = lax.all_gather(values_v, "dp", axis=0, tiled=True)
    rows_in = keys_in.shape[0]
    key_pos = jnp.arange(rows_in, dtype=jnp.int32)

    def compute(state):
        run_max, run_sum, run_acc = state
        scores = (
            jnp.einsum(
                "tgrd,sgd->tgrs",
                query_grp,
                keys_in.reshape(rows_in, KV_HEADS, HEAD),
                preferred_element_type=jnp.float32,
            )
            * score_scale
        )
        allowed = (key_pos[None, :] >= req_start[:, None]) & (key_pos[None, :] <= position[:, None])
        allowed = allowed[:, None, None, :]
        scores = jnp.where(allowed, scores, NEG_BIG)
        new_max = jnp.maximum(run_max, jnp.max(scores, axis=-1))
        weights = jnp.where(allowed, jnp.exp(scores - new_max[..., None]), 0.0)
        new_sum = jnp.sum(weights, axis=-1)
        mixed_vals = jnp.einsum(
            "tgrs,sgd->tgrd",
            weights.astype(jnp.bfloat16),
            vals_in.reshape(rows_in, KV_HEADS, HEAD),
            preferred_element_type=jnp.float32,
        )
        return (new_max, new_sum, mixed_vals)

    relevant = (first_row <= last_pos) & (first_row + rows_in - 1 >= first_start)
    run_max, run_sum, run_acc = lax.cond(relevant, compute, lambda state: state, init_state)
    attended = (run_acc / run_sum[..., None]).reshape(tok_count, q_width).astype(jnp.bfloat16)
    z_out = low_rank(attended, sel_in[:, :, rank_r : 2 * rank_r], slot_hot)
    residual = tokens.astype(jnp.float32) + jnp.dot(
        attended, w_out, preferred_element_type=jnp.float32
    )
    residual = residual + jnp.dot(
        z_out,
        sel_out[:, :, qkv_width : qkv_width + model_width].reshape(-1, model_width),
        preferred_element_type=jnp.float32,
    )
    residual = residual.astype(jnp.bfloat16)
    normed_two = rms_norm(residual, moe_gain)
    logits = jnp.dot(normed_two, w_router, preferred_element_type=jnp.float32)
    gate_weights = jax.nn.softmax(jnp.take_along_axis(logits, expert_ids, axis=1), axis=1)
    z_experts = low_rank(normed_two, sel_in[:, :, 2 * rank_r : 4 * rank_r], slot_hot)
    z_width = z_experts.shape[1]
    n_experts = exp_local * n_ep
    chosen = jnp.take(all_expert, adapter_ids.reshape(-1), axis=0).reshape(
        n_ep, n_requests, 3 * rank_r, ff_width
    )
    b_gate = chosen[:, :, 0:rank_r]
    b_up = chosen[:, :, rank_r : 2 * rank_r]
    blank_blk = jnp.zeros_like(b_gate)
    b_joint = jnp.concatenate(
        [jnp.concatenate([b_gate, blank_blk], axis=3), jnp.concatenate([blank_blk, b_up], axis=3)],
        axis=2,
    )
    b_joint = b_joint.reshape(n_ep, n_requests * 2 * rank_r, 2 * ff_width)
    a_down = jnp.transpose(chosen[:, :, 2 * rank_r : 3 * rank_r], (0, 3, 1, 2)).reshape(
        n_ep, ff_width, n_requests * rank_r
    )
    keep_mask = jnp.repeat(slot_hot, rank_r, axis=1)
    flat_expert = expert_ids.reshape(-1)
    earlier = earlier_counts(flat_expert, n_experts)
    slot_dest = flat_expert * CAP + earlier
    source_row = (
        jnp.full((n_experts * CAP,), tok_count, jnp.int32)
        .at[slot_dest]
        .set(jnp.arange(tok_count * top_count, dtype=jnp.int32) // top_count)
    )
    padded_x = jnp.concatenate([normed_two, jnp.zeros((1, model_width), jnp.bfloat16)])
    padded_z = jnp.concatenate([z_experts, jnp.zeros((1, z_width), jnp.bfloat16)])
    send_x = padded_x[source_row].reshape(n_ep, exp_local, CAP, model_width)
    send_z = padded_z[source_row].reshape(n_ep, exp_local, CAP, z_width)
    recv_x, recv_z = (
        lax.all_to_all(send_x, "ep", split_axis=0, concat_axis=0, tiled=True),
        lax.all_to_all(send_z, "ep", split_axis=0, concat_axis=0, tiled=True),
    )
    pre_act = jnp.einsum("jecd,edf->jecf", recv_x, w_gate_up, preferred_element_type=jnp.float32)
    pre_act = pre_act + jnp.einsum(
        "jecr,jrf->jecf", recv_z, b_joint, preferred_element_type=jnp.float32
    )
    hidden = (jax.nn.silu(pre_act[..., :ff_width]) * pre_act[..., ff_width:]).astype(jnp.bfloat16)
    expert_out = jnp.einsum(
        "jech,ehd->jecd", hidden, w_down, preferred_element_type=jnp.float32
    ).astype(jnp.bfloat16)
    down_coeff = jnp.einsum(
        "jech,jhr->jecr", hidden, a_down, preferred_element_type=jnp.float32
    ).astype(jnp.bfloat16)
    expert_out, down_coeff = (expert_out, down_coeff)
    back_out, back_coeff = (
        lax.all_to_all(expert_out, "ep", split_axis=0, concat_axis=0, tiled=True),
        lax.all_to_all(down_coeff, "ep", split_axis=0, concat_axis=0, tiled=True),
    )
    rows_out = back_out.reshape(n_experts * CAP, model_width)[slot_dest].reshape(
        tok_count, top_count, model_width
    )
    rows_coeff = back_coeff.reshape(n_experts * CAP, -1)[slot_dest].reshape(
        tok_count, top_count, -1
    )
    owner_hot = (expert_ids // exp_local)[:, :, None] == jnp.arange(n_ep, dtype=jnp.int32)[
        None, None, :
    ]
    weighted = jnp.where(owner_hot, gate_weights[:, :, None], 0.0)
    part_out = jnp.einsum(
        "tkg,tkd->tgd", weighted, rows_out.astype(jnp.float32), precision=lax.Precision.HIGHEST
    ).astype(jnp.bfloat16)
    part_coeff = jnp.einsum(
        "tkg,tkr->tgr", weighted, rows_coeff.astype(jnp.float32), precision=lax.Precision.HIGHEST
    ).astype(jnp.bfloat16)
    moe_sum = jnp.sum(part_out.astype(jnp.float32), axis=1)
    coeff_sum = jnp.sum(
        jnp.where(keep_mask[:, None, :], part_coeff.astype(jnp.float32), 0.0), axis=1
    ).astype(jnp.bfloat16)
    down_delta = jnp.dot(
        coeff_sum,
        sel_out[:, :, qkv_width + model_width : qkv_width + 2 * model_width].reshape(
            -1, model_width
        ),
        preferred_element_type=jnp.float32,
    )
    return (residual.astype(jnp.float32) + moe_sum + down_delta).astype(jnp.bfloat16)


def solution(mesh):
    return jax.shard_map(
        per_device,
        mesh=mesh,
        in_specs=(
            P(("ep", "dp"), None),
            P("ep", None),
            P(),
            P(("ep", "dp"), None),
            P(),
            P(),
            P(),
            P(),
            P(),
            P("ep", None, None),
            P("ep", None, None),
            P("dp", None, None),
            P("dp", None, None),
            P("dp", None, None),
        ),
        out_specs=P(("ep", "dp"), None),
        check_vma=False,
    )
```

profile of v0, /device:TPU:1, one launch (start us, length us, event | category | flops | bytes accessed | tf_op | source)
XLA Modules:
  0.0 616.2 jit_solution(15493466018963444724)
XLA Ops:
  12.8 5.0 fusion.72
  17.9 65.3 %all-gather.8.cloned.1.call-done = bf16[64,16,4096]{2,1,0:T(8,128)(2,1)} async-done(((bf16[4,16,4096]{2,1,0:T(8,128)(2,1)}), bf16[64,16,4096]{2,1,0:T(8,128)(2,1)}) %all-gather.8.cloned.1.call-update) | async-done | bytes 8388624 | tf_op jit(solution)/shard_map/all_gather | solution.py:101
  83.2 3.9 gather_fusion.1
  88.0 67.7 %all-gather.6.cloned.1.call-done = bf16[64,1024,64]{1,2,0:T(8,128)(2,1)} async-done(((bf16[4,1024,64]{1,2,0:T(8,128)(2,1)}), bf16[64,1024,64]{1,2,0:T(8,128)(2,1)}) %all-gather.6.cloned.1.call-update) | async-done | bytes 8388624 | tf_op jit(solution)/shard_map/all_gather | solution.py:100
  155.8 3.9 gather_fusion
  160.6 4.0 convolution_add_fusion
  164.6 2.0 slice.107
  166.5 2.0 copy.115
  170.4 1.8 slice.138
  179.1 15.9 %reduce-window.11 = s32[32,16,128]{2,1,0:T(8,128)S(1)} reduce-window(s32[32,16,128]{2,1,0:T(8,128)} %fusion.69, s32[]{:T(128)} %constant.130.clone.1), window={size=1x1x128 pad=0_0x0_0x127_0}, to_apply=%region_11.12 | reduce-window | flops 8323072 | bytes 524292 | tf_op jit(solution)/shard_map/reduce-window.1
  195.9 1.8 copy.147
  197.7 1.5 reduce-window.14
  200.9 8.2 %scatter_custom_fusion = s32[3072]{0:T(1024)S(1)} fusion(s32[2048]{0:T(1024)S(1)} %bitcast.173, s32[2048]{0:T(1024)} %add_select_fusion, s32[]{:T(128)} %constant.128.clone.1), kind=kCustom, calls=%fused_computation.129 | custom fusion | bytes 12800 | tf_op jit(solution)/shard_map/scatter | solution.py:201
  209.2 1.5 fusion.98
  210.7 1.4 copy.116
  212.1 1.4 subtract_convert_fusion
  213.5 12.3 %all-gather.10.cloned.1.call-done = bf16[4096,512]{0,1:T(8,128)(2,1)} async-done(((bf16[256,512]{0,1:T(8,128)(2,1)}), bf16[4096,512]{0,1:T(8,128)(2,1)}) %all-gather.10.cloned.1.call-update) | async-done | bytes 4194320 | tf_op jit(solution)/shard_map/all_gather | solution.py:131
  225.8 53.9 %all-gather.12.cloned.1.call-done = bf16[4096,512]{1,0:T(8,128)(2,1)} async-done(((bf16[256,512]{1,0:T(8,128)(2,1)}), bf16[4096,512]{1,0:T(8,128)(2,1)}) %all-gather.12.cloned.1.call-update) | async-done | bytes 4194320 | tf_op jit(solution)/shard_map/all_gather | solution.py:132
  279.7 88.2 %conditional.1 = (f32[256,8,2]{0,2,1:T(2,128)S(1)}, f32[256,8,2,64]{0,3,2,1:T(8,128)}) conditional(s32[]{:T(128)} %bitcast.12, () %tuple.13, (s32[4096]{0:T(1024)S(1)}, s32[4096]{0:T(1024)S(1)}, s32[256]{0:T(256)S(1)}, s32[256]{0:T(256)S(1)}, bf16[4096,512]{0,1:T(8,128)(2,1)}, /*index=5*/bf16[256,8,2,64]{0,3,2,1:T(8,128)(2,1)S(1)}, ...), branch_computations={%region_4.5_spmd, %region_5.8_spmd} | conditional | flops 4516212736 | bytes 224004112 | solution.py:162
  280.2 3.9 compare_and_fusion
  284.0 26.5 %fusion = (f32[256,8,2]{0,2,1:T(2,128)S(1)}, f32[8,4096,256,2]{2,1,3,0:T(8,128)}) fusion(pred[256,4096]{0,1:T(8,128)(4,1)} %compare_and_fusion, bf16[4096,8,64,1]{0,2,3,1:T(8,128)(2,1)} %bitcast.176, bf16[256,8,2,64]{0,3,2,1:T(8,128)(2,1)S(1)} %get-tuple-element.23), kind=kOutput, calls=%fused_computation.11 | convolution fusion | flops 2197811200 | bytes 72892416 | tf_op jit(solution)/shard_map/cond/branch_1_fun/tgrd,sgd->tgrs/dot_general | solution.py:139
  310.5 22.8 %fusion.2 = f32[256,8,2]{0,2,1:T(2,128)S(1)} fusion(f32[8,4096,256,2]{2,1,3,0:T(8,128)} %get-tuple-element.65, f32[256,8,2]{0,2,1:T(2,128)S(1)} %broadcast_maximum_fusion, pred[256,4096]{0,1:T(8,128)(4,1)} %compare_and_fusion), kind=kLoop, calls=%fused_computation.13 | loop fusion | flops 83881984 | bytes 68190208 | tf_op jit(solution)/shard_map/cond/branch_1_fun/reduce_sum | solution.py:152
  333.3 6.4 %copy.117 = bf16[4096,512]{0,1:T(8,128)(2,1)} copy(bf16[4096,512]{1,0:T(8,128)(2,1)} %get-tuple-element.63) | data formatting | bytes 8388608 | tf_op jit(solution)/shard_map
  339.7 28.1 %fusion.6 = f32[256,8,2,64]{0,3,2,1:T(8,128)} fusion(bf16[4096,8,64,1]{0,2,3,1:T(8,128)(2,1)} %bitcast.150, f32[8,4096,256,2]{2,1,3,0:T(8,128)} %get-tuple-element.65, f32[256,8,2]{0,2,1:T(2,128)S(1)} %broadcast_maximum_fusion, pred[256,4096]{0,1:T(8,128)(4,1)} %compare_and_fusion), kind=kOutput, calls=%fused_computation.17 | convolution fusion | flops 2231369728 | bytes 73416704 | tf_op jit(solution)/shard_map/cond/branch_1_fun/tgrs,sgd->tgrd/dot_general | solution.py:153
  367.8 1.3 divide_convert_fusion
  369.2 1.7 convert_add_fusion.1
  370.9 1.9 fusion.54
  373.1 14.0 %gather_fusion.2 = bf16[3072,1024]{1,0:T(8,128)(2,1)} fusion(bf16[257,1024]{1,0:T(8,128)(2,1)S(1)} %concatenate.32, s32[3072]{0:T(1024)S(1)} %fusion.77), kind=kCustom, calls=%fused_computation.2 | custom fusion | bytes 12595200 | tf_op jit(solution)/shard_map/gather | solution.py:205
  387.1 5.8 all-to-all-start
  393.3 2.5 gather_fusion.4
  397.6 9.2 %gather_fusion.3 = bf16[3072,64]{1,0:T(8,128)(2,1)S(1)} fusion(bf16[257,64]{1,0:T(8,128)(2,1)S(1)} %concatenate.33.clone, s32[3072]{0:T(1024)S(1)} %copy-done.11), kind=kCustom, calls=%fused_computation.3 | custom fusion | bytes 798720 | tf_op jit(solution)/shard_map/gather | solution.py:206
  407.9 56.4 %all-to-all-done = bf16[8,4,96,1024]{3,2,1,0:T(8,128)(2,1)} async-done(((bf16[8,4,96,1024]{3,2,1,0:T(8,128)(2,1)}), bf16[8,4,96,1024]{3,2,1,0:T(8,128)(2,1)}, u32[]{:S(2)}, u32[]{:S(2)}) %all-to-all-start) | async-done | bytes 6291488 | tf_op jit(solution)/shard_map/all_to_all | solution.py:208
  464.2 4.4 all-to-all-start.1
  468.6 13.8 %fusion.12 = f32[4,8,96,1024]{3,2,1,0:T(8,128)} fusion(bf16[4,1024,1024]{2,1,0:T(8,128)(2,1)} %param.25, bf16[8,4,96,1024]{3,2,1,0:T(8,128)(2,1)} %all-to-all-done), kind=kOutput, calls=%fused_computation.23 | convolution fusion | flops 6442450944 | bytes 27262976 | tf_op jit(solution)/shard_map/jecd,edf->jecf/dot_general | solution.py:211
  482.4 6.7 %bitcast_add_fusion = f32[8,4,96,1024]{3,2,0,1:T(8,128)S(1)} fusion(f32[4,8,96,1024]{3,2,1,0:T(8,128)} %fusion.12, bf16[8,64,1024,1]{2,1,0,3:T(8,128)(2,1)} %bitcast.149, bf16[8,4,96,64]{2,3,1,0:T(8,128)(2,1)S(1)} %all-to-all-done.1), kind=kOutput, calls=%fused_computation.22 | convolution fusion | flops 405798912 | bytes 26607616 | tf_op jit(solution)/shard_map/jecr,jrf->jecf/dot_general | solution.py:212
  489.2 2.1 fusion.14
  491.2 1.6 copy-done.4
  492.9 1.9 fusion.45
  494.8 4.8 all-to-all-start.3
  499.6 6.6 %convert_bitcast_fusion = bf16[8,4,96,1024]{3,2,0,1:T(8,128)(2,1)S(1)} fusion(bf16[8,4,96,512]{3,2,0,1:T(8,128)(2,1)} %copy-done.4, bf16[4,512,1024]{2,1,0:T(8,128)(2,1)} %param.26), kind=kOutput, calls=%fused_computation.29 | convolution fusion | flops 3224371200 | bytes 13631488 | tf_op jit(solution)/shard_map/jech,ehd->jecd/dot_general | solution.py:216
  506.2 3.3 copy.134
  509.6 5.2 all-to-all-start.2
  515.6 16.8 %gather_fusion.7 = f32[2048]{0:T(1024)S(1)} fusion(f32[256,32]{0,1:T(8,128)S(1)} %fusion.99, s32[2048]{0:T(1024)S(1)} %reshape.451), kind=kCustom, calls=%fused_computation.7 | custom fusion | bytes 32768 | tf_op jit(solution)/shard_map/jit(take_along_axis)/gather | solution.py:176
  533.1 6.2 %gather_fusion.6 = bf16[2048,32]{1,0:T(8,128)(2,1)S(1)} fusion(bf16[3072,32]{1,0:T(8,128)(2,1)S(1)} %bitcast.145, s32[2048]{0:T(1024)S(1)} %broadcast_clamp_fusion), kind=kCustom, calls=%fused_computation.6 | custom fusion | bytes 270336 | tf_op jit(solution)/shard_map/gather | solution.py:230
  539.3 1.3 fusion.42
  540.6 45.3 %all-to-all-done.2 = bf16[8,4,96,1024]{3,2,1,0:T(8,128)(2,1)} async-done(((bf16[8,4,96,1024]{3,2,1,0:T(8,128)(2,1)}), bf16[8,4,96,1024]{3,2,1,0:T(8,128)(2,1)}, u32[]{:S(2)}, u32[]{:S(2)}) %all-to-all-start.2) | async-done | bytes 6291488 | tf_op jit(solution)/shard_map/all_to_all | solution.py:224
  586.0 14.8 %gather_fusion.5 = bf16[2048,1024]{1,0:T(8,128)(2,1)} fusion(bf16[3072,1024]{1,0:T(8,128)(2,1)} %bitcast.48, s32[2048]{0:T(1024)S(1)} %broadcast_clamp_fusion), kind=kCustom, calls=%fused_computation.5 | custom fusion | bytes 8396800 | tf_op jit(solution)/shard_map/gather | solution.py:227
  600.8 7.5 %convert_reduce_fusion = f32[256,1024]{1,0:T(8,128)S(1)} fusion(bf16[2048,1024]{1,0:T(8,128)(2,1)} %gather_fusion.5, f32[256,8]{1,0:T(8,128)S(1)} %copy.121, s32[256,8]{1,0:T(8,128)S(1)} %copy.118), kind=kOutput, calls=%fused_computation.25 | convolution fusion | flops 207388672 | bytes 5259264 | tf_op jit(solution)/shard_map/tkg,tkd->tgd/dot_general | solution.py:237
  (140 shorter events, 23.7 us)
Async XLA Ops:
  6.5 362.6 %copy-start = (bf16[1024,1024]{1,0:T(8,128)(2,1)S(1)}, bf16[1024,1024]{1,0:T(8,128)(2,1)}, u32[]{:S(2)}) copy-start(bf16[1024,1024]{1,0:T(8,128)(2,1)} %param.22) | copy-start | bytes 6291460
  6.5 154.0 %copy-start.2 = (bf16[256,1024]{1,0:T(8,128)(2,1)S(1)}, bf16[256,1024]{1,0:T(8,128)(2,1)}, u32[]{:S(2)}) copy-start(bf16[256,1024]{1,0:T(8,128)(2,1)} %param.16) | copy-start | bytes 1572868
  6.5 76.7 %all-gather.8.cloned.1.call-start = ((), (), s32[]{:S(2)}) async-start(), calls=%async_computation.5 | async-start | bytes 8912896 | tf_op jit(solution)/shard_map/all_gather | solution.py:101
  7.3 148.5 %all-gather.6.cloned.1.call-start = ((), (), s32[]{:S(2)}) async-start(), calls=%async_computation.4 | async-start | bytes 8912896 | tf_op jit(solution)/shard_map/all_gather | solution.py:100
  8.0 217.8 %all-gather.10.cloned.1.call-start = ((), (), s32[]{:S(2)}) async-start(), calls=%async_computation.6 | async-start | bytes 4456448 | tf_op jit(solution)/shard_map/all_gather | solution.py:131
  10.5 162.4 %copy-start.22 = (s32[256]{0:T(256)}, s32[256]{0:T(256)S(1)}, u32[]{:S(2)}) copy-start(s32[256]{0:T(256)S(1)} %iota_add_fusion) | copy-start | bytes 3076
  11.3 162.2 %copy-start.19 = (s32[256]{0:T(256)}, s32[256]{0:T(256)S(1)}, u32[]{:S(2)}) copy-start(s32[256]{0:T(256)S(1)} %select_reduce_fusion) | copy-start | bytes 3076
  12.6 152.0 %copy-start.17 = (pred[256,2]{0,1:T(4,128)(4,1)}, pred[256,2]{0,1:T(4,128)(4,1)S(1)}, u32[]{:S(2)}) copy-start(pred[256,2]{0,1:T(4,128)(4,1)S(1)} %iota_compare_fusion.7) | copy-start | bytes 1540
  17.9 156.2 %copy-start.7 = (s32[256,8]{0,1:T(8,128)S(1)}, s32[256,8]{0,1:T(8,128)}, u32[]{:S(2)}) copy-start(s32[256,8]{0,1:T(8,128)} %param.19) | copy-start | bytes 24580
  87.2 89.8 %copy-start.24 = (bf16[1024]{0:T(1024)(128)(2,1)S(1)}, bf16[1024]{0:T(1024)(128)(2,1)}, u32[]{:S(2)}) copy-start(bf16[1024]{0:T(1024)(128)(2,1)} %param.23) | copy-start | bytes 6148
  87.3 0.7 copy-start.6
  159.8 0.7 copy-start.5
  164.6 46.1 %slice-start = ((f32[256,2048]{1,0:T(8,128)}), f32[256,1024]{1,0:T(8,128)S(1)}, s32[]{:S(2)}) async-start(f32[256,2048]{1,0:T(8,128)} %convolution_add_fusion), calls=%async_computation.9 | async-start | bytes 2097152 | tf_op jit(solution)/shard_map/slice | solution.py:113
  170.4 109.3 %all-gather.12.cloned.1.call-start = ((), (), s32[]{:S(2)}) async-start(), calls=%async_computation.7 | async-start | bytes 4456448 | tf_op jit(solution)/shard_map/all_gather | solution.py:132
  172.3 221.1 %all-gather.14.cloned.1.call-start = ((), (), s32[]{:S(2)}) async-start(), calls=%async_computation.8 | async-start | bytes 3342336 | tf_op jit(solution)/shard_map/all_gather | solution.py:102
  200.0 79.6 %copy-start.20 = (s32[256]{0:T(256)S(1)}, s32[256]{0:T(256)}, u32[]{:S(2)}) copy-start(s32[256]{0:T(256)} %copy-done.19) | copy-start | bytes 3076
  200.1 79.6 %copy-start.23 = (s32[256]{0:T(256)S(1)}, s32[256]{0:T(256)}, u32[]{:S(2)}) copy-start(s32[256]{0:T(256)} %copy-done.22) | copy-start | bytes 3076
  200.9 8.2 %copy-start.14 = (s32[2048,1]{0,1:T(1,128)}, s32[2048,1]{0,1:T(1,128)S(1)}, u32[]{:S(2)}) copy-start(s32[2048,1]{0,1:T(1,128)S(1)} %compare_select_fusion) | copy-start | bytes 24580
  209.2 164.0 %copy-start.10 = (s32[3072]{0:T(1024)}, s32[3072]{0:T(1024)S(1)}, u32[]{:S(2)}) copy-start(s32[3072]{0:T(1024)S(1)} %fusion.77) | copy-start | bytes 36868
  279.7 89.5 %copy-start.3 = (bf16[256,1024]{1,0:T(8,128)(2,1)S(1)}, bf16[256,1024]{1,0:T(8,128)(2,1)}, u32[]{:S(2)}) copy-start(bf16[256,1024]{1,0:T(8,128)(2,1)} %param.16) | copy-start | bytes 1572868
  367.8 5.0 copy-start.16
  387.1 5.8 copy-start.21
  387.1 77.1 %all-to-all-start = ((bf16[8,4,96,1024]{3,2,1,0:T(8,128)(2,1)}), bf16[8,4,96,1024]{3,2,1,0:T(8,128)(2,1)}, u32[]{:S(2)}, u32[]{:S(2)}) async-start(bf16[8,4,96,1024]{3,2,1,0:T(8,128)(2,1)} %bitcast.146), calls=%async_computation | async-start | bytes 12582912 | tf_op jit(solution)/shard_map/all_to_all | solution.py:208
  393.0 4.2 copy-start.18
  393.0 4.2 slice-start.1
  393.0 4.6 copy-start.11
  464.2 18.2 %all-to-all-start.1 = ((bf16[8,4,96,64]{2,3,1,0:T(8,128)(2,1)}), bf16[8,4,96,64]{2,3,1,0:T(8,128)(2,1)S(1)}, u32[]{:S(2)}, u32[]{:S(2)}) async-start(bf16[8,4,96,64]{2,3,1,0:T(8,128)(2,1)} %copy.130), calls=%async_computation.1 | async-start | bytes 1048576 | tf_op jit(solution)/shard_map/all_to_all | solution.py:209
  491.2 1.7 copy-start.4
  494.8 14.8 %all-to-all-start.3 = ((bf16[8,4,96,32]{2,3,1,0:T(8,128)(2,1)}), bf16[8,4,96,32]{2,3,1,0:T(8,128)(2,1)S(1)}, u32[]{:S(2)}, u32[]{:S(2)}) async-start(bf16[8,4,96,32]{2,3,1,0:T(8,128)(2,1)} %fusion.45), calls=%async_computation.3 | async-start | bytes 524288 | tf_op jit(solution)/shard_map/all_to_all | solution.py:225
  509.5 5.4 copy-start.8
  509.5 5.6 copy-start.13
  509.5 5.8 copy-start.15
  509.5 5.8 copy-start.12
  509.6 76.4 %all-to-all-start.2 = ((bf16[8,4,96,1024]{3,2,1,0:T(8,128)(2,1)}), bf16[8,4,96,1024]{3,2,1,0:T(8,128)(2,1)}, u32[]{:S(2)}, u32[]{:S(2)}) async-start(bf16[8,4,96,1024]{3,2,1,0:T(8,128)(2,1)} %copy.134), calls=%async_computation.2 | async-start | bytes 12582912 | tf_op jit(solution)/shard_map/all_to_all | solution.py:224
  586.0 22.4 %copy-start.9 = (bf16[2,16,1024]{2,1,0:T(8,128)(2,1)S(1)}, bf16[2,16,1024]{2,1,0:T(8,128)(2,1)}, u32[]{:S(2)}) copy-start(bf16[2,16,1024]{2,1,0:T(8,128)(2,1)} %get-tuple-element.76) | copy-start | bytes 196612
  586.0 23.4 %copy-start.1 = (bf16[1024,1024]{1,0:T(8,128)(2,1)S(1)}, bf16[1024,1024]{1,0:T(8,128)(2,1)}, u32[]{:S(2)}) copy-start(bf16[1024,1024]{1,0:T(8,128)(2,1)} %param.22) | copy-start | bytes 6291460
Sparse Core Ops, SparseCore 0:
  9.5 73.6 all-gather.7
  85.3 70.3 all-gather.5
  170.5 55.2 all-gather.9
  227.8 51.8 all-gather.11
  281.7 46.8 all-gather.13
where the time goes:
time: 623 us; the launch traced here: 616 us
  waiting for transfers between devices  303 us (49%)
  local copies, waits for them, and re-layouts  110 us (18%)
  matrix products  107 us (17%)
  other arithmetic  60.4 us (10%)
  starting transfers between devices  20.4 us (3%)
  between operations  15.4 us (2%)
    all_gather x1, waiting for transfers between devices, per_device(): lax.all_gather(adapter_in, 'dp', axis=0, tiled=True)  67.7 us
    all_gather x1, waiting for transfers between devices, per_device(): lax.all_gather(adapter_out, 'dp', axis=0, tiled=True)  65.3 us
    all_to_all x1, waiting for transfers between devices, per_device(): lax.all_to_all(send_x, 'ep', split_axis=0, concat_axis=0, tiled=True)  56.4 us
    all_gather x1, waiting for transfers between devices, per_device(): vals_in = lax.all_gather(values_v, 'dp', axis=0, tiled=True)  53.9 us
    all_to_all x1, waiting for transfers between devices, per_device(): lax.all_to_all(expert_out, 'ep', split_axis=0, concat_axis=0, tiled=True)  45.3 us
    dot_general x1, matrix products, compute(): jnp.einsum('tgrs,sgd->tgrd', weights.astype(jnp.bfloat16), vals_in.reshap...  28.1 us
    dot_general x1, matrix products, compute(): jnp.einsum('tgrd,sgd->tgrs', query_grp, keys_in.reshape(rows_in, KV_HEADS...  26.5 us
    reduce_sum x1, other arithmetic, compute(): new_sum = jnp.sum(weights, axis=-1)  22.8 us
  transfers between devices with their start and end apart: 9, of which 6 were waited for; matrix products, arithmetic and copies ran while one was open for 37% of the time, Pallas kernels for 0%

commit v1 on v0

v1 whole, which is shorter than its diff:
```python
import math

import jax
import jax.numpy as jnp
from jax import lax
from jax.experimental import pallas as pl
from jax.experimental.pallas import tpu as pltpu
from jax.sharding import PartitionSpec as P

HEADS = 16
KV_HEADS = 8
HEAD = 64
CAP = 96
TOK = 256
D = 1024
FF = 512
QKV = 2048
N_DP = 16
N_EP = 8
EXP_LOCAL = 4
PIECE = 160

EPS = 1e-06
THETA = 10000.0
NEG_BIG = -1e30

BF = jnp.bfloat16
F32 = jnp.float32
MESH = pl.DeviceIdType.MESH
NT = (((1,), (1,)), ((), ()))
TN = (((0,), (0,)), ((), ()))


def dot(a, b):
    return jnp.dot(a, b, preferred_element_type=F32)


def dot_nt(a, b):
    return lax.dot_general(a, b, NT, preferred_element_type=F32)


def dot_tn(a, b):
    return lax.dot_general(a, b, TN, preferred_element_type=F32)


def other(me, off, count):
    return lax.rem(me + off, count)


def barrier(axes):
    sem = pltpu.get_barrier_semaphore()
    total = 0
    for axis, count in axes:
        me = lax.axis_index(axis)
        for off in range(1, count):
            pl.semaphore_signal(
                sem, inc=1, device_id={axis: other(me, off, count)}, device_id_type=MESH
            )
        total += count - 1
    pl.semaphore_wait(sem, total)


def push(src, dst, send_sem, recv_sem, axis, peer):
    copy = pltpu.make_async_remote_copy(
        src_ref=src,
        dst_ref=dst,
        send_sem=send_sem,
        recv_sem=recv_sem,
        device_id={axis: peer},
        device_id_type=MESH,
    )
    copy.start()
    return copy


def norm_rows(floats, gain_row):
    meansq = jnp.mean(floats * floats, axis=-1, keepdims=True)
    return (floats * lax.rsqrt(meansq + EPS) * gain_row).astype(BF)


def first_request_rows(lengths_ref, first_pos):
    pos = first_pos + lax.broadcasted_iota(jnp.int32, (TOK, 1), 0)
    return pos < lengths_ref[0, 0]


def first_request_lanes(lengths_ref, first_pos):
    pos = first_pos + lax.broadcasted_iota(jnp.int32, (1, TOK), 1)
    return pos < lengths_ref[0, 0]


def masked_pair(z, use, in_first):
    lo = z[:, use * 16 : use * 16 + 16]
    hi = z[:, 64 + use * 16 : 64 + use * 16 + 16]
    return jnp.where(in_first, lo, 0.0).astype(BF), jnp.where(in_first, 0.0, hi).astype(BF)


def up_block(pair, adapters_ref, block):
    halves = []
    for half in range(2):
        row = 64 + 32 * half
        halves.append(
            dot(pair[0], adapters_ref[block, row : row + 16, :])
            + dot(pair[1], adapters_ref[block, row + 16 : row + 32, :])
        )
    return jnp.concatenate(halves, axis=1)


def project_kernel(
    lengths_ref, tok_ref, gain_ref, w_ref, contrib_ref, cos_ref, sin_ref,
    recv_ref, adapters_ref,
    gathered, normed_scr, send_scr, s1, r1, s2, r2, s3, r3,
):
    me = lax.axis_index("dp")
    barrier([("dp", N_DP)])
    first = []
    for off in range(1, N_DP):
        peer = other(me, off, N_DP)
        first.append(
            push(contrib_ref.at[peer], gathered.at[me], s1.at[off], r1.at[off], "dp", peer)
        )
    normed_scr[...] = norm_rows(tok_ref[...].astype(F32), gain_ref[...].astype(F32))
    total = contrib_ref[me].astype(F32)
    for copy in first:
        copy.wait()
    for off in range(1, N_DP):
        total = total + gathered[other(me, off, N_DP)].astype(F32)
    adapters_ref[me] = total.astype(BF)
    second = []
    for off in range(1, N_DP):
        peer = other(me, off, N_DP)
        second.append(
            push(adapters_ref.at[me], adapters_ref.at[me], s2.at[off], r2.at[off], "dp", peer)
        )
    for copy in second:
        copy.wait()
    in_first = first_request_rows(lengths_ref, me * TOK)
    normed = normed_scr[...]
    z = dot(normed, adapters_ref[:, 0:64, :].reshape(D, 128))
    pair = masked_pair(z, 0, in_first)
    cosine = cos_ref[...]
    sine = sin_ref[...]

    def rope(head_t, scale):
        a = head_t[0:32]
        b = head_t[32:64]
        return (
            ((a * cosine - b * sine) * scale).astype(BF),
            ((b * cosine + a * sine) * scale).astype(BF),
        )

    for block in range(8):
        cols = slice(block * 256, block * 256 + 256)
        p_t = (dot(normed, w_ref[:, cols]) + up_block(pair, adapters_ref, block)).T
        for sub in range(4):
            head_t = p_t[sub * 64 : sub * 64 + 64]
            if block < 4:
                head = block * 4 + sub
                a, b = rope(head_t, 0.125)
                send_scr[head, 0:32, :] = a
                send_scr[head, 32:64, :] = b
            elif block < 6:
                head = (block - 4) * 4 + sub
                a, b = rope(head_t, 1.0)
                for twin in range(2):
                    send_scr[2 * head + twin, 64:96, :] = a
                    send_scr[2 * head + twin, 96:128, :] = b
            else:
                head = (block - 6) * 4 + sub
                v = head_t.astype(BF)
                for twin in range(2):
                    send_scr[2 * head + twin, 128:192, :] = v
    third = []
    for off in range(1, N_DP):
        peer = other(me, off, N_DP)
        third.append(push(send_scr.at[peer], recv_ref.at[me], s3.at[off], r3.at[off], "dp", peer))
    recv_ref[me] = send_scr[me]
    for copy in third:
        copy.wait()


def attention_kernel(lengths_ref, qkv_ref, out_ref, k_scr):
    length = lengths_ref[0, 0]
    for block in range(N_DP):
        k_scr[block] = qkv_ref[block, 64:128, :].astype(F32).T.astype(BF)
    lanes = lax.broadcasted_iota(jnp.int32, (1, TOK), 1)
    subs = lax.broadcasted_iota(jnp.int32, (TOK, 1), 0)

    def query_block(qb, unused):
        q_t = qkv_ref[qb, 0:64, :]
        q_first = qb * TOK
        qpos = q_first + lanes
        start = jnp.where(qpos >= length, length, 0)
        lo = jnp.where(q_first >= length, length, 0) // TOK
        mid = jnp.where(q_first + TOK - 1 >= length, (length + TOK - 1) // TOK, 0)
        mid = jnp.minimum(mid, qb)

        def step(kb, state, masked):
            run_max, run_sum, acc = state
            scores = dot(k_scr[kb], q_t)
            if masked:
                kpos = kb * TOK + subs
                allowed = (kpos >= start) & (kpos <= qpos)
                scores = jnp.where(allowed, scores, NEG_BIG)
            new_max = jnp.maximum(run_max, jnp.max(scores, axis=0, keepdims=True))
            weights = jnp.exp(scores - new_max)
            if masked:
                weights = jnp.where(allowed, weights, 0.0)
            fade = jnp.exp(run_max - new_max)
            new_sum = run_sum * fade + jnp.sum(weights, axis=0, keepdims=True)
            new_acc = acc * fade + dot(qkv_ref[kb, 128:192, :], weights.astype(BF))
            return new_max, new_sum, new_acc

        state = (
            jnp.full((1, TOK), NEG_BIG, F32),
            jnp.zeros((1, TOK), F32),
            jnp.zeros((HEAD, TOK), F32),
        )
        state = lax.fori_loop(lo, mid, lambda kb, s: step(kb, s, True), state)
        state = lax.fori_loop(mid, qb, lambda kb, s: step(kb, s, False), state)
        run_max, run_sum, acc = step(qb, state, True)
        out_ref[qb] = (acc / run_sum).astype(BF)
        return unused

    lax.fori_loop(0, N_DP, query_block, 0)


def route_kernel(
    lengths_ref, att_ref, tok_ref, adapters_ref, w_ref, gain_ref, router_ref, ids_ref,
    res_ref, x_ref, z_ref, rw_ref, ea_ref,
    att_t, x_scr, z_scr, rw_scr, ea_scr, s1, r1, s2, r2,
):
    me = lax.axis_index("dp")
    ep = lax.axis_index("ep")
    barrier([("dp", N_DP), ("ep", N_EP)])
    first = []
    for off in range(1, N_DP):
        peer = other(me, off, N_DP)
        first.append(push(att_ref.at[peer], att_t.at[me], s1.at[off], r1.at[off], "dp", peer))
    att_t[me] = att_ref[me]
    for use in range(3):
        for cb in range(4):
            ea_scr[use * 32 : use * 32 + 32, cb * 128 : cb * 128 + 128] = adapters_ref[
                use * 4 + cb, 128:160, :
            ]
    in_first = first_request_rows(lengths_ref, me * TOK)
    lane_first = first_request_lanes(lengths_ref, me * TOK)
    a_all = adapters_ref[:, 0:64, :].reshape(D, 128)
    for copy in first:
        copy.wait()
    attended = att_t[...].reshape(D, TOK).astype(F32).T.astype(BF)
    pair = masked_pair(dot(attended, a_all), 1, in_first)
    delta = jnp.concatenate([up_block(pair, adapters_ref, 8 + b) for b in range(4)], axis=1)
    residual = (tok_ref[...].astype(F32) + dot(attended, w_ref[...]) + delta).astype(BF)
    res_ref[...] = residual
    normed = norm_rows(residual.astype(F32), gain_ref[...].astype(F32))
    x_scr[...] = normed
    logits = dot_nt(router_ref[...], normed)
    experts = lax.broadcasted_iota(jnp.int32, (32, TOK), 0)
    ids = ids_ref[...]
    chosen = experts == ids[0:1]
    for k in range(1, 8):
        chosen = chosen | (experts == ids[k : k + 1])
    top = jnp.max(jnp.where(chosen, logits, NEG_BIG), axis=0, keepdims=True)
    raised = jnp.where(chosen, jnp.exp(jnp.where(chosen, logits - top, 0.0)), 0.0)
    gates = raised / jnp.sum(raised, axis=0, keepdims=True)
    before = (
        lax.broadcasted_iota(jnp.int32, (TOK, TOK), 0)
        < lax.broadcasted_iota(jnp.int32, (TOK, TOK), 1)
    ).astype(F32).astype(BF)
    rank = jnp.where(chosen, dot(chosen.astype(F32).astype(BF), before), -1.0)
    for owner in range(N_EP):
        rw_scr[owner, 0:4, :] = rank[owner * 4 : owner * 4 + 4]
        rw_scr[owner, 4:8, :] = gates[owner * 4 : owner * 4 + 4]
    z_t = dot(normed, a_all).T
    for use in range(2):
        lo = z_t[32 + use * 16 : 48 + use * 16]
        hi = z_t[96 + use * 16 : 112 + use * 16]
        z_scr[use * 32 : use * 32 + 16, :] = jnp.where(lane_first, lo, 0.0).astype(BF)
        z_scr[use * 32 + 16 : use * 32 + 32, :] = jnp.where(lane_first, 0.0, hi).astype(BF)
    second = []
    for off in range(1, N_EP):
        peer = other(ep, off, N_EP)
        for a, (src, dst) in enumerate(
            [
                (x_scr, x_ref.at[ep]),
                (z_scr, z_ref.at[ep]),
                (rw_scr.at[peer], rw_ref.at[ep]),
                (ea_scr, ea_ref.at[ep]),
            ]
        ):
            second.append(push(src, dst, s2.at[a, off], r2.at[a, off], "ep", peer))
    x_ref[ep] = x_scr[...]
    z_ref[ep] = z_scr[...]
    rw_ref[ep] = rw_scr[ep]
    ea_ref[ep] = ea_scr[...]
    for copy in second:
        copy.wait()


def expert_kernel(
    x_ref, z_ref, rw_ref, ea_ref, w_up_ref, w_down_ref, part_ref, coeff_ref,
    rows_scr, hid_scr, acc, coeff_acc,
):
    e = pl.program_id(0)

    @pl.when(e == 0)
    def _():
        acc[...] = jnp.zeros_like(acc)
        coeff_acc[...] = jnp.zeros_like(coeff_acc)

    slots = lax.broadcasted_iota(jnp.int32, (CAP, TOK), 0).astype(F32)

    def picker(j):
        return rw_ref[j, pl.ds(e, 1), :] == slots

    def gather(j, unused):
        pick = picker(j).astype(F32).astype(BF)
        rows_scr[pl.ds(pl.multiple_of(j * CAP, CAP), CAP), :] = dot(pick, x_ref[j]).astype(BF)
        return unused

    lax.fori_loop(0, N_EP, gather, 0)
    group = 2 * CAP
    for g in range(N_EP // 2):
        rows = slice(g * group, g * group + group)
        pre_gate = dot(rows_scr[rows, :], w_up_ref[0, :, 0:FF])
        pre_up = dot(rows_scr[rows, :], w_up_ref[0, :, FF:])
        for sub in range(2):
            j = 2 * g + sub
            local = slice(sub * CAP, sub * CAP + CAP)
            hit = picker(j)
            pick = hit.astype(F32).astype(BF)
            zr = dot_nt(pick, z_ref[j]).astype(BF)
            gate = pre_gate[local] + dot(zr[:, 0:32], ea_ref[j, 0:32, :])
            up = pre_up[local] + dot(zr[:, 32:64], ea_ref[j, 32:64, :])
            hid_scr[j * CAP : j * CAP + CAP, :] = (jax.nn.silu(gate) * up).astype(BF)
        out = dot(hid_scr[rows, :], w_down_ref[0])
        for sub in range(2):
            j = 2 * g + sub
            local = slice(sub * CAP, sub * CAP + CAP)
            hit = picker(j)
            pick = hit.astype(F32).astype(BF)
            weight = jnp.sum(
                jnp.where(hit, rw_ref[j, pl.ds(e + 4, 1), :], 0.0), axis=1, keepdims=True
            )
            scaled = (out[local] * weight).astype(BF)
            coeff = dot_nt(hid_scr[j * CAP : j * CAP + CAP, :], ea_ref[j, 64:96, :])
            acc[j] += dot_tn(pick, scaled)
            coeff_acc[j] += dot_tn((coeff * weight).astype(BF), pick)

    @pl.when(e == EXP_LOCAL - 1)
    def _():
        part_ref[...] = acc[...].astype(BF)
        coeff_ref[...] = coeff_acc[...].astype(BF)


def combine_kernel(
    lengths_ref, part_ref, coeff_ref, res_ref, adapters_ref, out_ref,
    part_in, coeff_in, s1, r1,
):
    ep = lax.axis_index("ep")
    me = lax.axis_index("dp")
    barrier([("ep", N_EP)])
    copies = []
    for off in range(1, N_EP):
        peer = other(ep, off, N_EP)
        copies.append(push(part_ref.at[peer], part_in.at[ep], s1.at[0, off], r1.at[0, off], "ep", peer))
        copies.append(push(coeff_ref.at[peer], coeff_in.at[ep], s1.at[1, off], r1.at[1, off], "ep", peer))
    lane_first = first_request_lanes(lengths_ref, me * TOK)
    total = part_ref[ep].astype(F32)
    csum = coeff_ref[ep].astype(F32)
    for copy in copies:
        copy.wait()
    for off in range(1, N_EP):
        peer = other(ep, off, N_EP)
        total = total + part_in[peer].astype(F32)
        csum = csum + coeff_in[peer].astype(F32)
    low = jnp.where(lane_first, csum[0:16], 0.0).astype(BF)
    high = jnp.where(lane_first, 0.0, csum[16:32]).astype(BF)
    for block in range(4):
        for half in range(2):
            row = 64 + 32 * half
            delta = dot_tn(low, adapters_ref[12 + block, row : row + 16, :]) + dot_tn(
                high, adapters_ref[12 + block, row + 16 : row + 32, :]
            )
            cols = slice(block * 256 + half * 128, block * 256 + half * 128 + 128)
            out_ref[:, cols] = (
                res_ref[:, cols].astype(F32) + total[:, cols] + delta
            ).astype(BF)


def vmem():
    return pl.BlockSpec(memory_space=pltpu.VMEM)


def smem():
    return pl.BlockSpec(memory_space=pltpu.SMEM)


def params(collective):
    return pltpu.CompilerParams(collective_id=collective, has_side_effects=True)


def shape(dims, dtype=BF):
    return jax.ShapeDtypeStruct(dims, dtype)


def pick_adapter(bank, wanted, first):
    chosen = jnp.zeros_like(bank[0])
    for i in range(bank.shape[0]):
        chosen = jnp.where(wanted == first + i, bank[i], chosen)
    return chosen


def per_device(
    tokens, lengths, adapter_ids, expert_ids, attn_gain, w_qkv, w_out, moe_gain,
    w_router, w_gate_up, w_down, adapter_in, adapter_out, adapter_expert,
):
    group_idx = lax.axis_index("ep")
    row_idx = lax.axis_index("dp")
    group_ids = lax.dynamic_index_in_dim(adapter_ids, group_idx, 0, keepdims=False)
    first = row_idx * adapter_in.shape[0]
    a_cat = jnp.concatenate(
        [pick_adapter(adapter_in, group_ids[r], first) for r in range(2)], axis=1
    )
    b_cat = jnp.concatenate(
        [pick_adapter(adapter_out, group_ids[r], first) for r in range(2)], axis=0
    )
    e_cat = jnp.stack([pick_adapter(adapter_expert, group_ids[r], first) for r in range(2)])
    b_pieces = jnp.transpose(b_cat.reshape(32, 16, 2, 128), (1, 2, 0, 3)).reshape(16, 64, 128)
    e_pieces = jnp.transpose(e_cat.reshape(2, 3, 16, 4, 128), (1, 3, 0, 2, 4)).reshape(12, 32, 128)
    e_pieces = jnp.pad(e_pieces, ((0, 4), (0, 0), (0, 0)))
    contrib = jnp.concatenate([a_cat.reshape(16, 64, 128), b_pieces, e_pieces], axis=1)

    position = row_idx * TOK + jnp.arange(TOK, dtype=jnp.int32)
    rel_pos = position - jnp.where(position >= lengths[0, 0], lengths[0, 0], 0)
    half = HEAD // 2
    frequency = THETA ** (-jnp.arange(half, dtype=F32) / half)
    angles = rel_pos.astype(F32)[None, :] * frequency[:, None]
    cosine = jnp.cos(angles)
    sine = jnp.sin(angles)

    dma = pltpu.SemaphoreType.DMA
    qkv_in, adapters = pl.pallas_call(
        project_kernel,
        name="project",
        out_shape=(shape((N_DP, 192, TOK)), shape((N_DP, PIECE, 128))),
        in_specs=[smem()] + [vmem()] * 6,
        out_specs=(vmem(), vmem()),
        scratch_shapes=[
            pltpu.VMEM((N_DP, PIECE, 128), BF),
            pltpu.VMEM((TOK, D), BF),
            pltpu.VMEM((N_DP, 192, TOK), BF),
        ]
        + [dma((N_DP,))] * 6,
        compiler_params=params(0),
    )(lengths, tokens, attn_gain[None, :], w_qkv, contrib, cosine, sine)

    attended = pl.pallas_call(
        attention_kernel,
        name="attention",
        out_shape=shape((N_DP, HEAD, TOK)),
        in_specs=[smem(), vmem()],
        out_specs=vmem(),
        scratch_shapes=[pltpu.VMEM((N_DP, TOK, HEAD), BF)],
    )(lengths, qkv_in)

    residual, x_all, z_all, rw_all, ea_all = pl.pallas_call(
        route_kernel,
        name="route",
        out_shape=(
            shape((TOK, D)),
            shape((N_EP, TOK, D)),
            shape((N_EP, 64, TOK)),
            shape((N_EP, 8, TOK), F32),
            shape((N_EP, 96, FF)),
        ),
        in_specs=[smem()] + [vmem()] * 7,
        out_specs=(vmem(),) * 5,
        scratch_shapes=[
            pltpu.VMEM((N_DP, HEAD, TOK), BF),
            pltpu.VMEM((TOK, D), BF),
            pltpu.VMEM((64, TOK), BF),
            pltpu.VMEM((N_EP, 8, TOK), F32),
            pltpu.VMEM((96, FF), BF),
            dma((N_DP,)),
            dma((N_DP,)),
            dma((4, N_EP)),
            dma((4, N_EP)),
        ],
        compiler_params=params(1),
    )(
        lengths, attended, tokens, adapters, w_out, moe_gain[None, :],
        jnp.transpose(w_router), jnp.transpose(expert_ids),
    )

    def whole(dims):
        return pl.BlockSpec(dims, lambda e: (0,) * len(dims))

    parts, coeffs = pl.pallas_call(
        expert_kernel,
        name="experts",
        grid=(EXP_LOCAL,),
        out_shape=(shape((N_EP, TOK, D)), shape((N_EP, 32, TOK))),
        in_specs=[
            whole((N_EP, TOK, D)),
            whole((N_EP, 64, TOK)),
            whole((N_EP, 8, TOK)),
            whole((N_EP, 96, FF)),
            pl.BlockSpec((1, D, 2 * FF), lambda e: (e, 0, 0)),
            pl.BlockSpec((1, FF, D), lambda e: (e, 0, 0)),
        ],
        out_specs=(whole((N_EP, TOK, D)), whole((N_EP, 32, TOK))),
        scratch_shapes=[
            pltpu.VMEM((N_EP * CAP, D), BF),
            pltpu.VMEM((N_EP * CAP, FF), BF),
            pltpu.VMEM((N_EP, TOK, D), F32),
            pltpu.VMEM((N_EP, 32, TOK), F32),
        ],
    )(x_all, z_all, rw_all, ea_all, w_gate_up, w_down)

    return pl.pallas_call(
        combine_kernel,
        name="combine",
        out_shape=shape((TOK, D)),
        in_specs=[smem()] + [vmem()] * 4,
        out_specs=vmem(),
        scratch_shapes=[
            pltpu.VMEM((N_EP, TOK, D), BF),
            pltpu.VMEM((N_EP, 32, TOK), BF),
            dma((2, N_EP)),
            dma((2, N_EP)),
        ],
        compiler_params=params(2),
    )(lengths, parts, coeffs, residual, adapters)


def solution(mesh):
    return jax.shard_map(
        per_device,
        mesh=mesh,
        in_specs=(
            P(("ep", "dp"), None),
            P("ep", None),
            P(),
            P(("ep", "dp"), None),
            P(),
            P(),
            P(),
            P(),
            P(),
            P("ep", None, None),
            P("ep", None, None),
            P("dp", None, None),
            P("dp", None, None),
            P("dp", None, None),
        ),
        out_specs=P(("ep", "dp"), None),
        check_vma=False,
    )
```

time: 623 us -> 282 us (0.45); the launches traced: 616 us -> 282 us
  waiting for transfers between devices: 303 us -> 0 us
  Pallas kernels: 0 us -> 266 us
  matrix products: 107 us -> 0 us
  local copies, waits for them, and re-layouts: 110 us -> 7 us
  other arithmetic: 60.4 us -> 3.51 us
  starting transfers between devices: 20.4 us -> 0 us
  between operations: 15.4 us -> 5.28 us
    pallas_call x0 -> x5, Pallas kernels: none -> 266 us  [the longest x1 85.9 us: per_device(): pl.pallas_call(route_kernel, name='route', out_shape=(shape((TOK, D)), sh...]
    all_gather x5 -> x0, waiting for transfers between devices: 199 us -> none  [the longest x1 67.7 us: per_device(): lax.all_gather(adapter_in, 'dp', axis=0, tiled=True)]
    dot_general x15 -> x0, matrix products: 107 us -> none  [the longest x1 28.1 us: compute(): jnp.einsum('tgrs,sgd->tgrd', weights.astype(jnp.bfloat16), vals_in.reshap...]
    all_to_all x4 -> x0, waiting for transfers between devices: 102 us -> none  [the longest x1 56.4 us: per_device(): lax.all_to_all(send_x, 'ep', split_axis=0, concat_axis=0, tiled=True)]
    gather x12 -> x0, local copies, waits for them, and re-layouts: 71.7 us -> none  [the longest x5 17.2 us: per_device(): jnp.take_along_axis(logits, expert_ids, axis=1)]
    reduce_sum x6 -> x0, other arithmetic: 24.3 us -> none  [the longest x1 22.8 us: compute(): new_sum = jnp.sum(weights, axis=-1)]
    another operation x7 -> x1, other arithmetic: 21.6 us -> 0.01 us  [per_device(): jnp.stack([pick_adapter(adapter_expert, group_ids[r], first) for r in ran...]
    all_to_all x4 -> x0, starting transfers between devices: 20.2 us -> none  [the longest x1 5.83 us: per_device(): lax.all_to_all(send_x, 'ep', split_axis=0, concat_axis=0, tiled=True)]
  transfers between devices with their start and end apart: 9 -> 0, of which waited for: 6 -> 0; matrix products, arithmetic and copies ran while one was open for 37% -> 0% of each run, Pallas kernels for 0% -> 0%
where the time goes in v1:
time: 282 us
  Pallas kernels  266 us (94%)
  local copies, waits for them, and re-layouts  7 us (2%)
  between operations  5.28 us (2%)
  other arithmetic  3.51 us (1%)
    pallas_call x1, Pallas kernels, per_device(): pl.pallas_call(route_kernel, name='route', out_shape=(shape((TOK, D)), sh...  85.9 us
    pallas_call x1, Pallas kernels, per_device(): pl.pallas_call(combine_kernel, name='combine', out_shape=shape((TOK, D)),...  54.9 us
    pallas_call x1, Pallas kernels, per_device(): pl.pallas_call(project_kernel, name='project', out_shape=(shape((N_DP, 19...  50.9 us
    pallas_call x1, Pallas kernels, per_device(): pl.pallas_call(expert_kernel, name='experts', grid=(EXP_LOCAL,), out_shap...  39.8 us
    pallas_call x1, Pallas kernels, per_device(): pl.pallas_call(attention_kernel, name='attention', out_shape=shape((N_DP,...  34.7 us

profile of v1, /device:TPU:1, one launch (start us, length us, event | category | flops | bytes accessed | tf_op | source)
XLA Modules:
  0.0 282.0 jit_solution(7957089637331955451)
XLA Ops:
  0.0 0.0 copy-start
  0.0 0.0 copy-start.1
  0.0 0.7 copy-done
  0.7 0.1 constant_dynamic-slice_fusion
  0.8 0.5 fusion.4
  6.4 0.7 fusion.3
  7.1 1.3 broadcast_in_dim.14.gain_ref
  8.4 1.3 broadcast_in_dim.16.gain_ref
  9.7 0.8 multiply_sine_fusion
  10.5 0.9 select_select_fusion.5
  11.4 0.0 copy-start.2
  11.5 0.0 copy-done.1
  11.5 0.1 select_n.237
  11.6 0.1 copy.17
  11.7 0.1 select_n.246
  11.8 0.1 copy.18
  11.8 0.6 copy-done.2
  12.5 0.2 copy.15
  12.7 0.2 copy.16
  12.9 1.0 fusion.1.contrib_ref
  13.9 50.9 %project.1 = (bf16[16,192,256]{2,1,0:T(8,128)(2,1)}, bf16[16,160,128]{2,1,0:T(8,128)(2,1)}) custom-call(s32[1,2]{1,0:T(1,128)} %lengths_ref.7, bf16[256,1024]{1,0:T(8,128)(2,1)} %tok_ref.3, bf16[1,1024]{1,0:T(2,128)(2,1)} %broadcast_in_dim.14.gain_ref, bf16[1024,2048]{1,0:T(8,128)(2,1)} %w_ref.2, bf16[16,160,128]{2,1,0:T(8,128)(2,1)} %fusion.1.contrib_ref, ...), custom_call_target="tpu_custom_call" | custom-call | tf_op jit(solution)/shard_map/project/pallas_call | solution.py:443
  64.8 34.7 %attention.1.att_ref = bf16[16,64,256]{2,1,0:T(8,128)(2,1)} custom-call(s32[1,2]{1,0:T(1,128)} %lengths_ref.7, bf16[16,192,256]{2,1,0:T(8,128)(2,1)} %get-tuple-element.14.qkv_ref), custom_call_target="tpu_custom_call" | custom-call | tf_op jit(solution)/shard_map/attention/pallas_call | solution.py:458
  99.5 85.9 %route.1 = (bf16[256,1024]{1,0:T(8,128)(2,1)}, bf16[8,256,1024]{2,1,0:T(8,128)(2,1)}, bf16[8,64,256]{2,1,0:T(8,128)(2,1)}, f32[8,8,256]{2,1,0:T(8,128)}, bf16[8,96,512]{2,1,0:T(8,128)(2,1)}) custom-call(s32[1,2]{1,0:T(1,128)} %lengths_ref.7, bf16[16,64,256]{2,1,0:T(8,128)(2,1)} %attention.1.att_ref, bf16[256,1024]{1,0:T(8,128)(2,1)} %tok_ref.3, ...), custom_call_target="tpu_custom_call" | custom-call | tf_op jit(solution)/shard_map/route/pallas_call | solution.py:467
  185.5 39.8 %experts.1 = (bf16[8,256,1024]{2,1,0:T(8,128)(2,1)}, bf16[8,32,256]{2,1,0:T(8,128)(2,1)}) custom-call(bf16[8,256,1024]{2,1,0:T(8,128)(2,1)} %get-tuple-element.16.x_ref, bf16[8,64,256]{2,1,0:T(8,128)(2,1)} %get-tuple-element.17.z_ref, f32[8,8,256]{2,1,0:T(8,128)} %get-tuple-element.18.rw_ref, bf16[8,96,512]{2,1,0:T(8,128)(2,1)} %get-tuple-element.19.ea_ref, ...), custom_call_target="tpu_custom_call" | custom-call | tf_op jit(solution)/shard_map/experts/pallas_call | solution.py:499
  225.3 54.9 %combine.1 = bf16[256,1024]{1,0:T(8,128)(2,1)} custom-call(s32[1,2]{1,0:T(1,128)} %lengths_ref.7, bf16[8,256,1024]{2,1,0:T(8,128)(2,1)} %get-tuple-element.20.part_ref, bf16[8,32,256]{2,1,0:T(8,128)(2,1)} %get-tuple-element.21.coeff_ref, bf16[256,1024]{1,0:T(8,128)(2,1)} %get-tuple-element.22.res_ref, bf16[16,160,128]{2,1,0:T(8,128)(2,1)} %get-tuple-element.15.adapters_ref), custom_call_target="tpu_custom_call" | custom-call | tf_op jit(solution)/shard_map/combine/pallas_call | solution.py:521
  280.1 1.9 copy.22
  (9 shorter events, 0.2 us)
Async XLA Ops:
  0.0 0.7 copy-start
  0.0 11.5 %copy-start.1 = (bf16[4,16,4096]{2,1,0:T(8,128)(2,1)S(1)}, bf16[4,16,4096]{2,1,0:T(8,128)(2,1)}, u32[]{:S(2)}) copy-start(bf16[4,16,4096]{2,1,0:T(8,128)(2,1)} %param.26) | copy-start | bytes 1572868
  11.4 1.0 copy-start.2

commit v2 on v1

--- a/solution.py
+++ b/solution.py
@@ -71,6 +71,57 @@
     )
     copy.start()
     return copy
+
+
+def ring_ids(ep):
+    z = lax.div(ep, 2)
+    c = lax.rem(ep, 2)
+    up = lax.rem(z + 1, 4) * 2 + c
+    down = lax.rem(z + 3, 4) * 2 + c
+    far = lax.rem(z + 2, 4) * 2 + c
+    sib = z * 2 + 1 - c
+    return up, down, far, sib
+
+
+class RingGather:
+    def __init__(self, ep, src, dst, send, recv):
+        self.ep, self.src, self.dst, self.send, self.recv = ep, src, dst, send, recv
+        self.ids = ring_ids(ep)
+        self.half = src.shape[0] // 2
+        self.copies = []
+
+    def push(self, src, dst, peer):
+        i = len(self.copies)
+        self.copies.append(push(src, dst, self.send.at[i], self.recv.at[i], "ep", peer))
+
+    def start(self):
+        up, down, far, sib = self.ids
+        for peer in (up, down, sib):
+            self.push(self.src, self.dst.at[self.ep], peer)
+
+    def forward(self):
+        up, down, far, sib = self.ids
+        low, high = pl.ds(0, self.half), pl.ds(self.half, self.half)
+        self.copies[0].wait_recv()
+        self.push(self.dst.at[down, low], self.dst.at[down, low], up)
+        self.push(self.dst.at[down], self.dst.at[down], sib)
+        self.copies[1].wait_recv()
+        self.push(self.dst.at[up, high], self.dst.at[up, high], down)
+        self.push(self.dst.at[up], self.dst.at[up], sib)
+
+    def last(self):
+        up, down, far, sib = self.ids
+        low, high = pl.ds(0, self.half), pl.ds(self.half, self.half)
+        self.copies[3].wait_recv()
+        self.push(self.dst.at[far, low], self.dst.at[far, low], sib)
+        self.copies[5].wait_recv()
+        self.push(self.dst.at[far, high], self.dst.at[far, high], sib)
+
+    def finish(self):
+        for i, copy in enumerate(self.copies):
+            if i not in (0, 1, 3, 5):
+                copy.wait_recv()
+            copy.wait_send()
 
 
 def norm_rows(floats, gain_row):
@@ -227,7 +278,7 @@
 def route_kernel(
     lengths_ref, att_ref, tok_ref, adapters_ref, w_ref, gain_ref, router_ref, ids_ref,
     res_ref, x_ref, z_ref, rw_ref, ea_ref,
-    att_t, x_scr, z_scr, rw_scr, ea_scr, s1, r1, s2, r2,
+    att_t, x_scr, z_scr, rw_scr, ea_scr, s1, r1, s2, r2, s3, r3,
 ):
     me = lax.axis_index("dp")
     ep = lax.axis_index("ep")
@@ -242,6 +293,9 @@
             ea_scr[use * 32 : use * 32 + 32, cb * 128 : cb * 128 + 128] = adapters_ref[
                 use * 4 + cb, 128:160, :
             ]
+    ea_ring = RingGather(ep, ea_scr, ea_ref, s2.at[2], r2.at[2])
+    ea_ring.start()
+    ea_ref[ep] = ea_scr[...]
     in_first = first_request_rows(lengths_ref, me * TOK)
     lane_first = first_request_lanes(lengths_ref, me * TOK)
     a_all = adapters_ref[:, 0:64, :].reshape(D, 128)
@@ -277,22 +331,25 @@
         hi = z_t[96 + use * 16 : 112 + use * 16]
         z_scr[use * 32 : use * 32 + 16, :] = jnp.where(lane_first, lo, 0.0).astype(BF)
         z_scr[use * 32 + 16 : use * 32 + 32, :] = jnp.where(lane_first, 0.0, hi).astype(BF)
+    x_ring = RingGather(ep, x_scr, x_ref, s2.at[0], r2.at[0])
+    z_ring = RingGather(ep, z_scr, z_ref, s2.at[1], r2.at[1])
+    x_ring.start()
+    z_ring.start()
+    ea_ring.forward()
     second = []
     for off in range(1, N_EP):
         peer = other(ep, off, N_EP)
-        for a, (src, dst) in enumerate(
-            [
-                (x_scr, x_ref.at[ep]),
-                (z_scr, z_ref.at[ep]),
-                (rw_scr.at[peer], rw_ref.at[ep]),
-                (ea_scr, ea_ref.at[ep]),
-            ]
-        ):
-            second.append(push(src, dst, s2.at[a, off], r2.at[a, off], "ep", peer))
+        second.append(push(rw_scr.at[peer], rw_ref.at[ep], s3.at[off], r3.at[off], "ep", peer))
     x_ref[ep] = x_scr[...]
     z_ref[ep] = z_scr[...]
     rw_ref[ep] = rw_scr[ep]
-    ea_ref[ep] = ea_scr[...]
+    ea_ring.last()
+    x_ring.forward()
+    z_ring.forward()
+    x_ring.last()
+    z_ring.last()
+    for ring in (x_ring, z_ring, ea_ring):
+        ring.finish()
     for copy in second:
         copy.wait()
 
@@ -355,32 +412,66 @@
 
 def combine_kernel(
     lengths_ref, part_ref, coeff_ref, res_ref, adapters_ref, out_ref,
-    part_in, coeff_in, s1, r1,
+    sib_in, sums, far_in, near_in, coeff_in, s1, r1, s2, r2,
 ):
     ep = lax.axis_index("ep")
     me = lax.axis_index("dp")
     barrier([("ep", N_EP)])
+    up, down, far, sib = ring_ids(ep)
+    half = TOK // 2
+    low, high = pl.ds(0, half), pl.ds(half, half)
+    c = lax.rem(ep, 2)
+    order = [far, up, down, ep]
+    pairs = []
+    for i, dest in enumerate(order):
+        pairs.append(
+            push(part_ref.at[dest + 1 - 2 * c], sib_in.at[i], s1.at[i], r1.at[i], "ep", sib)
+        )
     copies = []
     for off in range(1, N_EP):
         peer = other(ep, off, N_EP)
-        copies.append(push(part_ref.at[peer], part_in.at[ep], s1.at[0, off], r1.at[0, off], "ep", peer))
-        copies.append(push(coeff_ref.at[peer], coeff_in.at[ep], s1.at[1, off], r1.at[1, off], "ep", peer))
+        copies.append(push(coeff_ref.at[peer], coeff_in.at[ep], s2.at[off], r2.at[off], "ep", peer))
+
+    def pair_sum(i):
+        pairs[i].wait_recv()
+        return part_ref[order[i]].astype(F32) + sib_in[i].astype(F32)
+
+    sums[0] = pair_sum(0).astype(BF)
+    hop = [
+        push(sums.at[0, low], far_in.at[0], s1.at[4], r1.at[4], "ep", up),
+        push(sums.at[0, high], far_in.at[1], s1.at[5], r1.at[5], "ep", down),
+    ]
+    up_sum = pair_sum(1)
+    sums[1, half:, :] = up_sum[half:].astype(BF)
+    hop.append(push(sums.at[1, high], near_in.at[0, high], s1.at[6], r1.at[6], "ep", up))
+    down_sum = pair_sum(2)
+    sums[2, 0:half, :] = down_sum[0:half].astype(BF)
+    hop.append(push(sums.at[2, low], near_in.at[1, low], s1.at[7], r1.at[7], "ep", down))
+    hop[0].wait_recv()
+    sums[1, 0:half, :] = (up_sum[0:half] + far_in[0].astype(F32)).astype(BF)
+    hop.append(push(sums.at[1, low], near_in.at[0, low], s1.at[8], r1.at[8], "ep", up))
+    hop[1].wait_recv()
+    sums[2, half:, :] = (down_sum[half:] + far_in[1].astype(F32)).astype(BF)
+    hop.append(push(sums.at[2, high], near_in.at[1, high], s1.at[9], r1.at[9], "ep", down))
     lane_first = first_request_lanes(lengths_ref, me * TOK)
-    total = part_ref[ep].astype(F32)
+    total = pair_sum(3)
     csum = coeff_ref[ep].astype(F32)
     for copy in copies:
         copy.wait()
     for off in range(1, N_EP):
-        peer = other(ep, off, N_EP)
-        total = total + part_in[peer].astype(F32)
-        csum = csum + coeff_in[peer].astype(F32)
-    low = jnp.where(lane_first, csum[0:16], 0.0).astype(BF)
-    high = jnp.where(lane_first, 0.0, csum[16:32]).astype(BF)
+        csum = csum + coeff_in[other(ep, off, N_EP)].astype(F32)
+    for copy in hop[2:]:
+        copy.wait_recv()
+    total = total + near_in[0].astype(F32) + near_in[1].astype(F32)
+    for copy in pairs + hop:
+        copy.wait_send()
+    lo_rows = jnp.where(lane_first, csum[0:16], 0.0).astype(BF)
+    hi_rows = jnp.where(lane_first, 0.0, csum[16:32]).astype(BF)
     for block in range(4):
         for half in range(2):
             row = 64 + 32 * half
-            delta = dot_tn(low, adapters_ref[12 + block, row : row + 16, :]) + dot_tn(
-                high, adapters_ref[12 + block, row + 16 : row + 32, :]
+            delta = dot_tn(lo_rows, adapters_ref[12 + block, row : row + 16, :]) + dot_tn(
+                hi_rows, adapters_ref[12 + block, row + 16 : row + 32, :]
             )
             cols = slice(block * 256 + half * 128, block * 256 + half * 128 + 128)
             out_ref[:, cols] = (
@@ -484,8 +575,10 @@
             pltpu.VMEM((96, FF), BF),
             dma((N_DP,)),
             dma((N_DP,)),
-            dma((4, N_EP)),
-            dma((4, N_EP)),
+            dma((3, 9)),
+            dma((3, 9)),
+            dma((N_EP,)),
+            dma((N_EP,)),
         ],
         compiler_params=params(1),
     )(
@@ -525,10 +618,15 @@
         in_specs=[smem()] + [vmem()] * 4,
         out_specs=vmem(),
         scratch_shapes=[
-            pltpu.VMEM((N_EP, TOK, D), BF),
+            pltpu.VMEM((4, TOK, D), BF),
+            pltpu.VMEM((3, TOK, D), BF),
+            pltpu.VMEM((2, TOK // 2, D), BF),
+            pltpu.VMEM((2, TOK, D), BF),
             pltpu.VMEM((N_EP, 32, TOK), BF),
-            dma((2, N_EP)),
-            dma((2, N_EP)),
+            dma((10,)),
+            dma((10,)),
+            dma((N_EP,)),
+            dma((N_EP,)),
         ],
         compiler_params=params(2),
     )(lengths, parts, coeffs, residual, adapters)

time: 282 us -> 219 us (0.78)
  Pallas kernels: 266 us -> 203 us
    pallas_call x1, Pallas kernels: 85.9 us -> 48.1 us  [per_device(): pl.pallas_call(route_kernel, name='route', out_shape=(shape((TOK, D)), sh...]
    pallas_call x1, Pallas kernels: 54.9 us -> 27.1 us  [per_device(): pl.pallas_call(combine_kernel, name='combine', out_shape=shape((TOK, D)),...]
where the time goes in v2:
time: 219 us
  Pallas kernels  203 us (93%)
  local copies, waits for them, and re-layouts  7 us (3%)
  between operations  5.28 us (2%)
  other arithmetic  3.51 us (2%)
    pallas_call x1, Pallas kernels, per_device(): pl.pallas_call(project_kernel, name='project', out_shape=(shape((N_DP, 19...  50.9 us
    pallas_call x1, Pallas kernels, per_device(): pl.pallas_call(route_kernel, name='route', out_shape=(shape((TOK, D)), sh...  48.1 us
    pallas_call x1, Pallas kernels, per_device(): pl.pallas_call(expert_kernel, name='experts', grid=(EXP_LOCAL,), out_shap...  39.8 us
    pallas_call x1, Pallas kernels, per_device(): pl.pallas_call(attention_kernel, name='attention', out_shape=shape((N_DP,...  37.1 us
    pallas_call x1, Pallas kernels, per_device(): pl.pallas_call(combine_kernel, name='combine', out_shape=shape((TOK, D)),...  27.1 us

profile of v2, /device:TPU:1, one launch (start us, length us, event | category | flops | bytes accessed | tf_op | source)
XLA Modules:
  0.0 218.7 jit_solution(6527648734537749817)
XLA Ops:
  0.0 0.0 copy-start
  0.0 0.0 copy-start.1
  0.0 0.7 copy-done
  0.7 0.1 constant_dynamic-slice_fusion
  0.8 0.5 fusion.4
  6.4 0.7 fusion.3
  7.1 1.3 broadcast_in_dim.14.gain_ref
  8.4 1.3 broadcast_in_dim.16.gain_ref
  9.7 0.8 multiply_sine_fusion
  10.5 0.9 select_select_fusion.5
  11.4 0.0 copy-start.2
  11.5 0.0 copy-done.1
  11.5 0.1 select_n.237
  11.6 0.1 copy.17
  11.7 0.1 select_n.246
  11.8 0.1 copy.18
  11.8 0.6 copy-done.2
  12.5 0.2 copy.15
  12.7 0.2 copy.16
  12.9 1.0 fusion.1.contrib_ref
  13.9 50.9 %project.1 = (bf16[16,192,256]{2,1,0:T(8,128)(2,1)}, bf16[16,160,128]{2,1,0:T(8,128)(2,1)}) custom-call(s32[1,2]{1,0:T(1,128)} %lengths_ref.7, bf16[256,1024]{1,0:T(8,128)(2,1)} %tok_ref.3, bf16[1,1024]{1,0:T(2,128)(2,1)} %broadcast_in_dim.14.gain_ref, bf16[1024,2048]{1,0:T(8,128)(2,1)} %w_ref.2, bf16[16,160,128]{2,1,0:T(8,128)(2,1)} %fusion.1.contrib_ref, ...), custom_call_target="tpu_custom_call" | custom-call | tf_op jit(solution)/shard_map/project/pallas_call | solution.py:534
  64.8 37.1 %attention.1.att_ref = bf16[16,64,256]{2,1,0:T(8,128)(2,1)} custom-call(s32[1,2]{1,0:T(1,128)} %lengths_ref.7, bf16[16,192,256]{2,1,0:T(8,128)(2,1)} %get-tuple-element.14.qkv_ref), custom_call_target="tpu_custom_call" | custom-call | tf_op jit(solution)/shard_map/attention/pallas_call | solution.py:549
  101.9 48.1 %route.1 = (bf16[256,1024]{1,0:T(8,128)(2,1)}, bf16[8,256,1024]{2,1,0:T(8,128)(2,1)}, bf16[8,64,256]{2,1,0:T(8,128)(2,1)}, f32[8,8,256]{2,1,0:T(8,128)}, bf16[8,96,512]{2,1,0:T(8,128)(2,1)}) custom-call(s32[1,2]{1,0:T(1,128)} %lengths_ref.7, bf16[16,64,256]{2,1,0:T(8,128)(2,1)} %attention.1.att_ref, bf16[256,1024]{1,0:T(8,128)(2,1)} %tok_ref.3, ...), custom_call_target="tpu_custom_call" | custom-call | tf_op jit(solution)/shard_map/route/pallas_call | solution.py:558
  150.0 39.8 %experts.1 = (bf16[8,256,1024]{2,1,0:T(8,128)(2,1)}, bf16[8,32,256]{2,1,0:T(8,128)(2,1)}) custom-call(bf16[8,256,1024]{2,1,0:T(8,128)(2,1)} %get-tuple-element.16.x_ref, bf16[8,64,256]{2,1,0:T(8,128)(2,1)} %get-tuple-element.17.z_ref, f32[8,8,256]{2,1,0:T(8,128)} %get-tuple-element.18.rw_ref, bf16[8,96,512]{2,1,0:T(8,128)(2,1)} %get-tuple-element.19.ea_ref, ...), custom_call_target="tpu_custom_call" | custom-call | tf_op jit(solution)/shard_map/experts/pallas_call | solution.py:592
  189.7 27.1 %combine.1 = bf16[256,1024]{1,0:T(8,128)(2,1)} custom-call(s32[1,2]{1,0:T(1,128)} %lengths_ref.7, bf16[8,256,1024]{2,1,0:T(8,128)(2,1)} %get-tuple-element.20.part_ref, bf16[8,32,256]{2,1,0:T(8,128)(2,1)} %get-tuple-element.21.coeff_ref, bf16[256,1024]{1,0:T(8,128)(2,1)} %get-tuple-element.22.res_ref, bf16[16,160,128]{2,1,0:T(8,128)(2,1)} %get-tuple-element.15.adapters_ref), custom_call_target="tpu_custom_call" | custom-call | tf_op jit(solution)/shard_map/combine/pallas_call | solution.py:614
  216.8 1.9 copy.22
  (9 shorter events, 0.2 us)
Async XLA Ops:
  0.0 0.7 copy-start
  0.0 11.5 %copy-start.1 = (bf16[4,16,4096]{2,1,0:T(8,128)(2,1)S(1)}, bf16[4,16,4096]{2,1,0:T(8,128)(2,1)}, u32[]{:S(2)}) copy-start(bf16[4,16,4096]{2,1,0:T(8,128)(2,1)} %param.26) | copy-start | bytes 1572868
  11.4 1.0 copy-start.2

commit v3 on v2

--- a/solution.py
+++ b/solution.py
@@ -18,7 +18,8 @@
 N_DP = 16
 N_EP = 8
 EXP_LOCAL = 4
-PIECE = 160
+AQ = 512
+AK = 512
 
 EPS = 1e-06
 THETA = 10000.0
@@ -47,7 +48,7 @@
     return lax.rem(me + off, count)
 
 
-def barrier(axes):
+def greet(axes):
     sem = pltpu.get_barrier_semaphore()
     total = 0
     for axis, count in axes:
@@ -57,6 +58,11 @@
                 sem, inc=1, device_id={axis: other(me, off, count)}, device_id_type=MESH
             )
         total += count - 1
+    return sem, total
+
+
+def barrier(axes):
+    sem, total = greet(axes)
     pl.semaphore_wait(sem, total)
 
 
@@ -145,51 +151,94 @@
     return jnp.where(in_first, lo, 0.0).astype(BF), jnp.where(in_first, 0.0, hi).astype(BF)
 
 
-def up_block(pair, adapters_ref, block):
-    halves = []
-    for half in range(2):
-        row = 64 + 32 * half
-        halves.append(
-            dot(pair[0], adapters_ref[block, row : row + 16, :])
-            + dot(pair[1], adapters_ref[block, row + 16 : row + 32, :])
-        )
-    return jnp.concatenate(halves, axis=1)
+def up_block(pair, pieces_ref, block, row):
+    return dot(pair[0], pieces_ref[block, row : row + 16, :]) + dot(
+        pair[1], pieces_ref[block, row + 16 : row + 32, :]
+    )
+
+
+def exchange(src, dst, send_sem, recv_sem, me, rows=None):
+    copies = []
+    for off in range(1, N_DP):
+        peer = other(me, off, N_DP)
+        from_ref, to_ref = src.at[peer], dst.at[me]
+        if rows is not None:
+            from_ref, to_ref = src.at[peer, rows], dst.at[me, rows]
+        copies.append(push(from_ref, to_ref, send_sem.at[off], recv_sem.at[off], "dp", peer))
+    return copies
+
+
+def sum_pieces(own_ref, gathered, me):
+    total = own_ref[me].astype(F32)
+    for off in range(1, N_DP):
+        total = total + gathered[other(me, off, N_DP)].astype(F32)
+    return total.astype(BF)
+
+
+def share(ref, send_sem, recv_sem, me):
+    copies = []
+    for off in range(1, N_DP):
+        peer = other(me, off, N_DP)
+        copies.append(push(ref.at[me], ref.at[me], send_sem.at[off], recv_sem.at[off], "dp", peer))
+    return copies
 
 
 def project_kernel(
-    lengths_ref, tok_ref, gain_ref, w_ref, contrib_ref, cos_ref, sin_ref,
-    recv_ref, adapters_ref,
-    gathered, normed_scr, send_scr, s1, r1, s2, r2, s3, r3,
+    lengths_ref, ids_ref, tok_ref, gain_ref, w_ref, in_bank, out_bank, exp_bank, freq_ref,
+    recv_ref, main_ref, rest_ref,
+    main_own, rest_own, main_in, rest_in, normed_scr, base_scr, send_scr,
+    s1, r1, s2, r2, s3, r3, s4, r4, s5, r5, s6, r6,
 ):
     me = lax.axis_index("dp")
-    barrier([("dp", N_DP)])
-    first = []
-    for off in range(1, N_DP):
-        peer = other(me, off, N_DP)
-        first.append(
-            push(contrib_ref.at[peer], gathered.at[me], s1.at[off], r1.at[off], "dp", peer)
-        )
-    normed_scr[...] = norm_rows(tok_ref[...].astype(F32), gain_ref[...].astype(F32))
-    total = contrib_ref[me].astype(F32)
-    for copy in first:
+    ep = lax.axis_index("ep")
+    greeted, expected = greet([("dp", N_DP)])
+    for p in range(12, N_DP):
+        rest_own[p, 32:64, :] = jnp.zeros((32, 128), BF)
+    halves = []
+    for r in range(2):
+        local = ids_ref[ep, r] - me * 4
+        held = (local >= 0) & (local < 4)
+        at = jnp.clip(local, 0, 3)
+        halves.append(jnp.where(held, in_bank[at].astype(F32), 0.0))
+        out_rows = jnp.where(held, out_bank[at].astype(F32), 0.0).astype(BF)
+        exp_rows = jnp.where(held, exp_bank[at].astype(F32), 0.0).astype(BF)
+        rows = slice(16 * r, 16 * r + 16)
+        for p in range(N_DP):
+            main_own[p, 64 + 16 * r : 80 + 16 * r, :] = out_rows[:, p * 128 : p * 128 + 128]
+            rest_own[p, rows, :] = out_rows[:, QKV + p * 128 : QKV + p * 128 + 128]
+        for use in range(3):
+            for cb in range(4):
+                rest_own[use * 4 + cb, 32 + 16 * r : 48 + 16 * r, :] = exp_rows[
+                    use * 16 : use * 16 + 16, cb * 128 : cb * 128 + 128
+                ]
+    a_cat = jnp.concatenate(halves, axis=1).astype(BF)
+    for p in range(N_DP):
+        main_own[p, 0:64, :] = a_cat[p * 64 : p * 64 + 64]
+    pl.semaphore_wait(greeted, expected)
+    main_1 = exchange(main_own, main_in, s1, r1, me)
+    rest_1 = exchange(rest_own, rest_in, s2, r2, me)
+    normed = norm_rows(tok_ref[...].astype(F32), gain_ref[...].astype(F32)[None, :])
+    normed_scr[...] = normed
+    base_scr[:, D:] = dot(normed, w_ref[:, D:])
+    pos = me * TOK + lax.broadcasted_iota(jnp.int32, (1, TOK), 1)
+    rel_pos = (pos - jnp.where(pos >= lengths_ref[0, 0], lengths_ref[0, 0], 0)).astype(F32)
+    angles = freq_ref[...] * rel_pos
+    cosine = jnp.cos(angles)
+    sine = jnp.sin(angles)
+    for copy in main_1:
         copy.wait()
-    for off in range(1, N_DP):
-        total = total + gathered[other(me, off, N_DP)].astype(F32)
-    adapters_ref[me] = total.astype(BF)
-    second = []
-    for off in range(1, N_DP):
-        peer = other(me, off, N_DP)
-        second.append(
-            push(adapters_ref.at[me], adapters_ref.at[me], s2.at[off], r2.at[off], "dp", peer)
-        )
-    for copy in second:
+    main_ref[me] = sum_pieces(main_own, main_in, me)
+    main_2 = share(main_ref, s3, r3, me)
+    base_scr[:, 0:D] = dot(normed_scr[...], w_ref[:, 0:D])
+    for copy in rest_1:
         copy.wait()
+    rest_ref[me] = sum_pieces(rest_own, rest_in, me)
+    rest_2 = share(rest_ref, s4, r4, me)
     in_first = first_request_rows(lengths_ref, me * TOK)
-    normed = normed_scr[...]
-    z = dot(normed, adapters_ref[:, 0:64, :].reshape(D, 128))
+    for copy in main_2:
+        copy.wait()
+    z = dot(normed_scr[...], main_ref[:, 0:64, :].reshape(D, 128))
     pair = masked_pair(z, 0, in_first)
-    cosine = cos_ref[...]
-    sine = sin_ref[...]
 
     def rope(head_t, scale):
         a = head_t[0:32]
@@ -199,57 +248,61 @@
             ((b * cosine + a * sine) * scale).astype(BF),
         )
 
+    def heads_of(block):
+        cols = slice(block * 128, block * 128 + 128)
+        p_t = (base_scr[:, cols] + up_block(pair, main_ref, block, 64)).T
+        return p_t[0:64], p_t[64:128]
+
+    for block in range(8, 12):
+        for sub, head_t in enumerate(heads_of(block)):
+            head = (block - 8) * 2 + sub
+            a, b = rope(head_t, 1.0)
+            for twin in range(2):
+                send_scr[2 * head + twin, 64:96, :] = a
+                send_scr[2 * head + twin, 96:128, :] = b
+    for block in range(12, 16):
+        for sub, head_t in enumerate(heads_of(block)):
+            head = (block - 12) * 2 + sub
+            v = head_t.astype(BF)
+            for twin in range(2):
+                send_scr[2 * head + twin, 128:192, :] = v
+    kv = exchange(send_scr, recv_ref, s5, r5, me, pl.ds(64, 128))
     for block in range(8):
-        cols = slice(block * 256, block * 256 + 256)
-        p_t = (dot(normed, w_ref[:, cols]) + up_block(pair, adapters_ref, block)).T
-        for sub in range(4):
-            head_t = p_t[sub * 64 : sub * 64 + 64]
-            if block < 4:
-                head = block * 4 + sub
-                a, b = rope(head_t, 0.125)
-                send_scr[head, 0:32, :] = a
-                send_scr[head, 32:64, :] = b
-            elif block < 6:
-                head = (block - 4) * 4 + sub
-                a, b = rope(head_t, 1.0)
-                for twin in range(2):
-                    send_scr[2 * head + twin, 64:96, :] = a
-                    send_scr[2 * head + twin, 96:128, :] = b
-            else:
-                head = (block - 6) * 4 + sub
-                v = head_t.astype(BF)
-                for twin in range(2):
-                    send_scr[2 * head + twin, 128:192, :] = v
-    third = []
-    for off in range(1, N_DP):
-        peer = other(me, off, N_DP)
-        third.append(push(send_scr.at[peer], recv_ref.at[me], s3.at[off], r3.at[off], "dp", peer))
+        for sub, head_t in enumerate(heads_of(block)):
+            head = block * 2 + sub
+            a, b = rope(head_t, 0.125)
+            send_scr[head, 0:32, :] = a
+            send_scr[head, 32:64, :] = b
+    q = exchange(send_scr, recv_ref, s6, r6, me, pl.ds(0, 64))
     recv_ref[me] = send_scr[me]
-    for copy in third:
+    for copy in rest_2 + kv + q:
         copy.wait()
 
 
 def attention_kernel(lengths_ref, qkv_ref, out_ref, k_scr):
     length = lengths_ref[0, 0]
     for block in range(N_DP):
-        k_scr[block] = qkv_ref[block, 64:128, :].astype(F32).T.astype(BF)
-    lanes = lax.broadcasted_iota(jnp.int32, (1, TOK), 1)
-    subs = lax.broadcasted_iota(jnp.int32, (TOK, 1), 0)
+        rows = slice(block * TOK, block * TOK + TOK)
+        k_scr[rows, :] = qkv_ref[block, 64:128, :].astype(F32).T.astype(BF)
+    nq = AQ // TOK
+    nk = AK // TOK
+    lanes = lax.broadcasted_iota(jnp.int32, (1, AQ), 1)
+    subs = lax.broadcasted_iota(jnp.int32, (AK, 1), 0)
 
     def query_block(qb, unused):
-        q_t = qkv_ref[qb, 0:64, :]
-        q_first = qb * TOK
+        q_t = jnp.concatenate([qkv_ref[qb * nq + i, 0:64, :] for i in range(nq)], axis=1)
+        q_first = qb * AQ
         qpos = q_first + lanes
         start = jnp.where(qpos >= length, length, 0)
-        lo = jnp.where(q_first >= length, length, 0) // TOK
-        mid = jnp.where(q_first + TOK - 1 >= length, (length + TOK - 1) // TOK, 0)
+        lo = jnp.where(q_first >= length, length, 0) // AK
+        mid = jnp.where(q_first + AQ - 1 >= length, (length + AK - 1) // AK, 0)
         mid = jnp.minimum(mid, qb)
 
         def step(kb, state, masked):
             run_max, run_sum, acc = state
-            scores = dot(k_scr[kb], q_t)
+            scores = dot(k_scr[pl.ds(pl.multiple_of(kb * AK, AK), AK), :], q_t)
             if masked:
-                kpos = kb * TOK + subs
+                kpos = kb * AK + subs
                 allowed = (kpos >= start) & (kpos <= qpos)
                 scores = jnp.where(allowed, scores, NEG_BIG)
             new_max = jnp.maximum(run_max, jnp.max(scores, axis=0, keepdims=True))
@@ -258,25 +311,32 @@
                 weights = jnp.where(allowed, weights, 0.0)
             fade = jnp.exp(run_max - new_max)
             new_sum = run_sum * fade + jnp.sum(weights, axis=0, keepdims=True)
-            new_acc = acc * fade + dot(qkv_ref[kb, 128:192, :], weights.astype(BF))
+            low = weights.astype(BF)
+            new_acc = acc * fade
+            for i in range(nk):
+                new_acc = new_acc + dot(
+                    qkv_ref[kb * nk + i, 128:192, :], low[i * TOK : i * TOK + TOK]
+                )
             return new_max, new_sum, new_acc
 
         state = (
-            jnp.full((1, TOK), NEG_BIG, F32),
-            jnp.zeros((1, TOK), F32),
-            jnp.zeros((HEAD, TOK), F32),
+            jnp.full((1, AQ), NEG_BIG, F32),
+            jnp.zeros((1, AQ), F32),
+            jnp.zeros((HEAD, AQ), F32),
         )
         state = lax.fori_loop(lo, mid, lambda kb, s: step(kb, s, True), state)
         state = lax.fori_loop(mid, qb, lambda kb, s: step(kb, s, False), state)
         run_max, run_sum, acc = step(qb, state, True)
-        out_ref[qb] = (acc / run_sum).astype(BF)
+        out = (acc / run_sum).astype(BF)
+        for i in range(nq):
+            out_ref[qb * nq + i] = out[:, i * TOK : i * TOK + TOK]
         return unused
 
-    lax.fori_loop(0, N_DP, query_block, 0)
+    lax.fori_loop(0, N_DP // nq, query_block, 0)
 
 
 def route_kernel(
-    lengths_ref, att_ref, tok_ref, adapters_ref, w_ref, gain_ref, router_ref, ids_ref,
+    lengths_ref, att_ref, tok_ref, main_ref, rest_ref, w_ref, gain_ref, router_ref, ids_ref,
     res_ref, x_ref, z_ref, rw_ref, ea_ref,
     att_t, x_scr, z_scr, rw_scr, ea_scr, s1, r1, s2, r2, s3, r3,
 ):
@@ -290,23 +350,23 @@
     att_t[me] = att_ref[me]
     for use in range(3):
         for cb in range(4):
-            ea_scr[use * 32 : use * 32 + 32, cb * 128 : cb * 128 + 128] = adapters_ref[
-                use * 4 + cb, 128:160, :
+            ea_scr[use * 32 : use * 32 + 32, cb * 128 : cb * 128 + 128] = rest_ref[
+                use * 4 + cb, 32:64, :
             ]
     ea_ring = RingGather(ep, ea_scr, ea_ref, s2.at[2], r2.at[2])
     ea_ring.start()
     ea_ref[ep] = ea_scr[...]
     in_first = first_request_rows(lengths_ref, me * TOK)
     lane_first = first_request_lanes(lengths_ref, me * TOK)
-    a_all = adapters_ref[:, 0:64, :].reshape(D, 128)
+    a_all = main_ref[:, 0:64, :].reshape(D, 128)
     for copy in first:
         copy.wait()
     attended = att_t[...].reshape(D, TOK).astype(F32).T.astype(BF)
     pair = masked_pair(dot(attended, a_all), 1, in_first)
-    delta = jnp.concatenate([up_block(pair, adapters_ref, 8 + b) for b in range(4)], axis=1)
+    delta = jnp.concatenate([up_block(pair, rest_ref, b, 0) for b in range(8)], axis=1)
     residual = (tok_ref[...].astype(F32) + dot(attended, w_ref[...]) + delta).astype(BF)
     res_ref[...] = residual
-    normed = norm_rows(residual.astype(F32), gain_ref[...].astype(F32))
+    normed = norm_rows(residual.astype(F32), gain_ref[...].astype(F32)[None, :])
     x_scr[...] = normed
     logits = dot_nt(router_ref[...], normed)
     experts = lax.broadcasted_iota(jnp.int32, (32, TOK), 0)
@@ -356,62 +416,52 @@
 
 def expert_kernel(
     x_ref, z_ref, rw_ref, ea_ref, w_up_ref, w_down_ref, part_ref, coeff_ref,
-    rows_scr, hid_scr, acc, coeff_acc,
+    rows_scr, z_scr, hid_scr, scaled_scr, cs_scr,
 ):
     e = pl.program_id(0)
-
-    @pl.when(e == 0)
-    def _():
-        acc[...] = jnp.zeros_like(acc)
-        coeff_acc[...] = jnp.zeros_like(coeff_acc)
-
     slots = lax.broadcasted_iota(jnp.int32, (CAP, TOK), 0).astype(F32)
-
-    def picker(j):
-        return rw_ref[j, pl.ds(e, 1), :] == slots
-
-    def gather(j, unused):
-        pick = picker(j).astype(F32).astype(BF)
-        rows_scr[pl.ds(pl.multiple_of(j * CAP, CAP), CAP), :] = dot(pick, x_ref[j]).astype(BF)
-        return unused
-
-    lax.fori_loop(0, N_EP, gather, 0)
-    group = 2 * CAP
-    for g in range(N_EP // 2):
-        rows = slice(g * group, g * group + group)
-        pre_gate = dot(rows_scr[rows, :], w_up_ref[0, :, 0:FF])
-        pre_up = dot(rows_scr[rows, :], w_up_ref[0, :, FF:])
-        for sub in range(2):
-            j = 2 * g + sub
-            local = slice(sub * CAP, sub * CAP + CAP)
-            hit = picker(j)
-            pick = hit.astype(F32).astype(BF)
-            zr = dot_nt(pick, z_ref[j]).astype(BF)
-            gate = pre_gate[local] + dot(zr[:, 0:32], ea_ref[j, 0:32, :])
-            up = pre_up[local] + dot(zr[:, 32:64], ea_ref[j, 32:64, :])
-            hid_scr[j * CAP : j * CAP + CAP, :] = (jax.nn.silu(gate) * up).astype(BF)
-        out = dot(hid_scr[rows, :], w_down_ref[0])
-        for sub in range(2):
-            j = 2 * g + sub
-            local = slice(sub * CAP, sub * CAP + CAP)
-            hit = picker(j)
-            pick = hit.astype(F32).astype(BF)
+    for j in range(N_EP):
+        pick = (rw_ref[j, pl.ds(e, 1), :] == slots).astype(F32).astype(BF)
+        rs = slice(j * CAP, j * CAP + CAP)
+        rows_scr[rs, :] = dot(pick, x_ref[j]).astype(BF)
+        z_scr[rs, :] = dot_nt(pick, z_ref[j]).astype(BF)
+    for f in range(2):
+        gate_cols = slice(f * 256, f * 256 + 256)
+        up_cols = slice(FF + f * 256, FF + f * 256 + 256)
+        pre_gate = dot(rows_scr[...], w_up_ref[0, :, gate_cols])
+        pre_up = dot(rows_scr[...], w_up_ref[0, :, up_cols])
+        for j in range(N_EP):
+            rs = slice(j * CAP, j * CAP + CAP)
+            gate = pre_gate[rs] + dot(z_scr[rs, 0:32], ea_ref[j, 0:32, gate_cols])
+            up = pre_up[rs] + dot(z_scr[rs, 32:64], ea_ref[j, 32:64, gate_cols])
+            hid_scr[rs, gate_cols] = (jax.nn.silu(gate) * up).astype(BF)
+    for f in range(4):
+        cols = slice(f * 256, f * 256 + 256)
+        out = dot(hid_scr[...], w_down_ref[0, :, cols])
+        for j in range(N_EP):
+            rs = slice(j * CAP, j * CAP + CAP)
+            hit = rw_ref[j, pl.ds(e, 1), :] == slots
             weight = jnp.sum(
                 jnp.where(hit, rw_ref[j, pl.ds(e + 4, 1), :], 0.0), axis=1, keepdims=True
             )
-            scaled = (out[local] * weight).astype(BF)
-            coeff = dot_nt(hid_scr[j * CAP : j * CAP + CAP, :], ea_ref[j, 64:96, :])
-            acc[j] += dot_tn(pick, scaled)
-            coeff_acc[j] += dot_tn((coeff * weight).astype(BF), pick)
+            scaled_scr[j, e, :, cols] = (out[rs] * weight).astype(BF)
+            if f == 0:
+                coeff = dot_nt(hid_scr[rs, :], ea_ref[j, 64:96, :])
+                cs_scr[j, e] = (coeff * weight).astype(BF)
 
     @pl.when(e == EXP_LOCAL - 1)
     def _():
-        part_ref[...] = acc[...].astype(BF)
-        coeff_ref[...] = coeff_acc[...].astype(BF)
+        for j in range(N_EP):
+            pick = jnp.concatenate(
+                [(rw_ref[j, i : i + 1, :] == slots).astype(F32).astype(BF) for i in range(4)],
+                axis=0,
+            )
+            part_ref[j] = dot_tn(pick, scaled_scr[j].reshape(4 * CAP, D)).astype(BF)
+            coeff_ref[j] = dot_tn(cs_scr[j].reshape(4 * CAP, 32), pick).astype(BF)
 
 
 def combine_kernel(
-    lengths_ref, part_ref, coeff_ref, res_ref, adapters_ref, out_ref,
+    lengths_ref, part_ref, coeff_ref, res_ref, rest_ref, out_ref,
     sib_in, sums, far_in, near_in, coeff_in, s1, r1, s2, r2,
 ):
     ep = lax.axis_index("ep")
@@ -467,16 +517,12 @@
         copy.wait_send()
     lo_rows = jnp.where(lane_first, csum[0:16], 0.0).astype(BF)
     hi_rows = jnp.where(lane_first, 0.0, csum[16:32]).astype(BF)
-    for block in range(4):
-        for half in range(2):
-            row = 64 + 32 * half
-            delta = dot_tn(lo_rows, adapters_ref[12 + block, row : row + 16, :]) + dot_tn(
-                hi_rows, adapters_ref[12 + block, row + 16 : row + 32, :]
-            )
-            cols = slice(block * 256 + half * 128, block * 256 + half * 128 + 128)
-            out_ref[:, cols] = (
-                res_ref[:, cols].astype(F32) + total[:, cols] + delta
-            ).astype(BF)
+    for block in range(8):
+        delta = dot_tn(lo_rows, rest_ref[8 + block, 0:16, :]) + dot_tn(
+            hi_rows, rest_ref[8 + block, 16:32, :]
+        )
+        cols = slice(block * 128, block * 128 + 128)
+        out_ref[:, cols] = (res_ref[:, cols].astype(F32) + total[:, cols] + delta).astype(BF)
 
 
 def vmem():
@@ -493,58 +539,40 @@
 
 def shape(dims, dtype=BF):
     return jax.ShapeDtypeStruct(dims, dtype)
-
-
-def pick_adapter(bank, wanted, first):
-    chosen = jnp.zeros_like(bank[0])
-    for i in range(bank.shape[0]):
-        chosen = jnp.where(wanted == first + i, bank[i], chosen)
-    return chosen
 
 
 def per_device(
     tokens, lengths, adapter_ids, expert_ids, attn_gain, w_qkv, w_out, moe_gain,
     w_router, w_gate_up, w_down, adapter_in, adapter_out, adapter_expert,
 ):
-    group_idx = lax.axis_index("ep")
-    row_idx = lax.axis_index("dp")
-    group_ids = lax.dynamic_index_in_dim(adapter_ids, group_idx, 0, keepdims=False)
-    first = row_idx * adapter_in.shape[0]
-    a_cat = jnp.concatenate(
-        [pick_adapter(adapter_in, group_ids[r], first) for r in range(2)], axis=1
-    )
-    b_cat = jnp.concatenate(
-        [pick_adapter(adapter_out, group_ids[r], first) for r in range(2)], axis=0
-    )
-    e_cat = jnp.stack([pick_adapter(adapter_expert, group_ids[r], first) for r in range(2)])
-    b_pieces = jnp.transpose(b_cat.reshape(32, 16, 2, 128), (1, 2, 0, 3)).reshape(16, 64, 128)
-    e_pieces = jnp.transpose(e_cat.reshape(2, 3, 16, 4, 128), (1, 3, 0, 2, 4)).reshape(12, 32, 128)
-    e_pieces = jnp.pad(e_pieces, ((0, 4), (0, 0), (0, 0)))
-    contrib = jnp.concatenate([a_cat.reshape(16, 64, 128), b_pieces, e_pieces], axis=1)
-
-    position = row_idx * TOK + jnp.arange(TOK, dtype=jnp.int32)
-    rel_pos = position - jnp.where(position >= lengths[0, 0], lengths[0, 0], 0)
     half = HEAD // 2
     frequency = THETA ** (-jnp.arange(half, dtype=F32) / half)
-    angles = rel_pos.astype(F32)[None, :] * frequency[:, None]
-    cosine = jnp.cos(angles)
-    sine = jnp.sin(angles)
-
     dma = pltpu.SemaphoreType.DMA
-    qkv_in, adapters = pl.pallas_call(
+    qkv_in, main, rest = pl.pallas_call(
         project_kernel,
         name="project",
-        out_shape=(shape((N_DP, 192, TOK)), shape((N_DP, PIECE, 128))),
-        in_specs=[smem()] + [vmem()] * 6,
-        out_specs=(vmem(), vmem()),
+        out_shape=(
+            shape((N_DP, 192, TOK)),
+            shape((N_DP, 96, 128)),
+            shape((N_DP, 64, 128)),
+        ),
+        in_specs=[smem(), smem()] + [vmem()] * 7,
+        out_specs=(vmem(),) * 3,
         scratch_shapes=[
-            pltpu.VMEM((N_DP, PIECE, 128), BF),
+            pltpu.VMEM((N_DP, 96, 128), BF),
+            pltpu.VMEM((N_DP, 64, 128), BF),
+            pltpu.VMEM((N_DP, 96, 128), BF),
+            pltpu.VMEM((N_DP, 64, 128), BF),
             pltpu.VMEM((TOK, D), BF),
+            pltpu.VMEM((TOK, QKV), F32),
             pltpu.VMEM((N_DP, 192, TOK), BF),
         ]
-        + [dma((N_DP,))] * 6,
+        + [dma((N_DP,))] * 12,
         compiler_params=params(0),
-    )(lengths, tokens, attn_gain[None, :], w_qkv, contrib, cosine, sine)
+    )(
+        lengths, adapter_ids, tokens, attn_gain, w_qkv, adapter_in, adapter_out,
+        adapter_expert, frequency[:, None],
+    )
 
     attended = pl.pallas_call(
         attention_kernel,
@@ -552,7 +580,7 @@
         out_shape=shape((N_DP, HEAD, TOK)),
         in_specs=[smem(), vmem()],
         out_specs=vmem(),
-        scratch_shapes=[pltpu.VMEM((N_DP, TOK, HEAD), BF)],
+        scratch_shapes=[pltpu.VMEM((N_DP * TOK, HEAD), BF)],
     )(lengths, qkv_in)
 
     residual, x_all, z_all, rw_all, ea_all = pl.pallas_call(
@@ -565,7 +593,7 @@
             shape((N_EP, 8, TOK), F32),
             shape((N_EP, 96, FF)),
         ),
-        in_specs=[smem()] + [vmem()] * 7,
+        in_specs=[smem()] + [vmem()] * 8,
         out_specs=(vmem(),) * 5,
         scratch_shapes=[
             pltpu.VMEM((N_DP, HEAD, TOK), BF),
@@ -582,7 +610,7 @@
         ],
         compiler_params=params(1),
     )(
-        lengths, attended, tokens, adapters, w_out, moe_gain[None, :],
+        lengths, attended, tokens, main, rest, w_out, moe_gain,
         jnp.transpose(w_router), jnp.transpose(expert_ids),
     )
 
@@ -605,9 +633,10 @@
         out_specs=(whole((N_EP, TOK, D)), whole((N_EP, 32, TOK))),
         scratch_shapes=[
             pltpu.VMEM((N_EP * CAP, D), BF),
+            pltpu.VMEM((N_EP * CAP, 64), BF),
             pltpu.VMEM((N_EP * CAP, FF), BF),
-            pltpu.VMEM((N_EP, TOK, D), F32),
-            pltpu.VMEM((N_EP, 32, TOK), F32),
+            pltpu.VMEM((N_EP, EXP_LOCAL, CAP, D), BF),
+            pltpu.VMEM((N_EP, EXP_LOCAL, CAP, 32), BF),
         ],
     )(x_all, z_all, rw_all, ea_all, w_gate_up, w_down)
 
@@ -629,7 +658,7 @@
             dma((N_EP,)),
         ],
         compiler_params=params(2),
-    )(lengths, parts, coeffs, residual, adapters)
+    )(lengths, parts, coeffs, residual, rest)
 
 
 def solution(mesh):

time: 219 us -> 171 us (0.78)
  Pallas kernels: 203 us -> 165 us
  between operations: 5.28 us -> 0.03 us
  other arithmetic: 3.51 us -> 0.62 us
    pallas_call x1, Pallas kernels: 37.1 us -> 22 us  [per_device(): pl.pallas_call(attention_kernel, name='attention', out_shape=shape((N_DP,...]
    pallas_call x1, Pallas kernels: 39.8 us -> 24.9 us  [per_device(): pl.pallas_call(expert_kernel, name='experts', grid=(EXP_LOCAL,), out_shap...]
    pallas_call x1, Pallas kernels: 50.9 us -> 45.7 us  [per_device(): pl.pallas_call(project_kernel, name='project', out_shape=(shape((N_DP, 19...]
    pallas_call x1, Pallas kernels: 48.1 us -> 45.2 us  [per_device(): pl.pallas_call(route_kernel, name='route', out_shape=(shape((TOK, D)), sh...]
    broadcast_in_dim x2 -> x0, local copies, waits for them, and re-layouts: 2.55 us -> none  [the longest x1 1.28 us: per_device(): moe_gain[None, :]]
    unnamed x7 -> x3, local copies, waits for them, and re-layouts: 3.18 us -> 5.57 us
where the time goes in v3:
time: 171 us
  Pallas kernels  165 us (96%)
  local copies, waits for them, and re-layouts  5.57 us (3%)
    pallas_call x1, Pallas kernels, per_device(): pl.pallas_call(project_kernel, name='project', out_shape=(shape((N_DP, 19...  45.7 us
    pallas_call x1, Pallas kernels, per_device(): pl.pallas_call(route_kernel, name='route', out_shape=(shape((TOK, D)), sh...  45.2 us
    pallas_call x1, Pallas kernels, per_device(): pl.pallas_call(combine_kernel, name='combine', out_shape=shape((TOK, D)),...  26.8 us
    pallas_call x1, Pallas kernels, per_device(): pl.pallas_call(expert_kernel, name='experts', grid=(EXP_LOCAL,), out_shap...  24.9 us
    pallas_call x1, Pallas kernels, per_device(): pl.pallas_call(attention_kernel, name='attention', out_shape=shape((N_DP,...  22 us
    unnamed x3, local copies, waits for them, and re-layouts  5.57 us

profile of v3, /device:TPU:1, one launch (start us, length us, event | category | flops | bytes accessed | tf_op | source)
XLA Modules:
  0.0 170.7 jit_solution(5581253094254395835)
XLA Ops:
  0.0 1.3 copy.15.ids_ref
  1.3 0.6 multiply_power_fusion.freq_ref
  2.0 2.4 %copy.16.in_bank = bf16[4,1024,64]{2,1,0:T(8,128)(2,1)} copy(bf16[4,1024,64]{1,2,0:T(8,128)(2,1)} %param.25) | data formatting | bytes 1048576 | tf_op args[11]
  4.3 45.7 %project.1 = (bf16[16,192,256]{2,1,0:T(8,128)(2,1)}, bf16[16,96,128]{2,1,0:T(8,128)(2,1)}, bf16[16,64,128]{2,1,0:T(8,128)(2,1)}) custom-call(s32[1,2]{1,0:T(1,128)} %lengths_ref.7, s32[8,2]{1,0:T(8,128)} %copy.15.ids_ref, bf16[256,1024]{1,0:T(8,128)(2,1)} %tok_ref.3, bf16[1024]{0:T(1024)(128)(2,1)} %gain_ref.2, bf16[1024,2048]{1,0:T(8,128)(2,1)} %w_ref.2, ...), custom_call_target="tpu_custom_call" | custom-call | tf_op jit(solution)/shard_map/project/pallas_call | solution.py:551
  50.0 22.0 %attention.1.att_ref = bf16[16,64,256]{2,1,0:T(8,128)(2,1)} custom-call(s32[1,2]{1,0:T(1,128)} %lengths_ref.7, bf16[16,192,256]{2,1,0:T(8,128)(2,1)} %get-tuple-element.15.qkv_ref), custom_call_target="tpu_custom_call" | custom-call | tf_op jit(solution)/shard_map/attention/pallas_call | solution.py:577
  71.9 45.2 %route.1 = (bf16[256,1024]{1,0:T(8,128)(2,1)}, bf16[8,256,1024]{2,1,0:T(8,128)(2,1)}, bf16[8,64,256]{2,1,0:T(8,128)(2,1)}, f32[8,8,256]{2,1,0:T(8,128)}, bf16[8,96,512]{2,1,0:T(8,128)(2,1)}) custom-call(s32[1,2]{1,0:T(1,128)} %lengths_ref.7, bf16[16,64,256]{2,1,0:T(8,128)(2,1)} %attention.1.att_ref, bf16[256,1024]{1,0:T(8,128)(2,1)} %tok_ref.3, ...), custom_call_target="tpu_custom_call" | custom-call | tf_op jit(solution)/shard_map/route/pallas_call | solution.py:586
  117.1 24.9 %experts.1 = (bf16[8,256,1024]{2,1,0:T(8,128)(2,1)}, bf16[8,32,256]{2,1,0:T(8,128)(2,1)}) custom-call(bf16[8,256,1024]{2,1,0:T(8,128)(2,1)} %get-tuple-element.18.x_ref, bf16[8,64,256]{2,1,0:T(8,128)(2,1)} %get-tuple-element.19.z_ref, f32[8,8,256]{2,1,0:T(8,128)} %get-tuple-element.20.rw_ref, bf16[8,96,512]{2,1,0:T(8,128)(2,1)} %get-tuple-element.21.ea_ref, ...), custom_call_target="tpu_custom_call" | custom-call | tf_op jit(solution)/shard_map/experts/pallas_call | solution.py:620
  142.0 26.8 %combine.1 = bf16[256,1024]{1,0:T(8,128)(2,1)} custom-call(s32[1,2]{1,0:T(1,128)} %lengths_ref.7, bf16[8,256,1024]{2,1,0:T(8,128)(2,1)} %get-tuple-element.22.part_ref, bf16[8,32,256]{2,1,0:T(8,128)(2,1)} %get-tuple-element.23.coeff_ref, bf16[256,1024]{1,0:T(8,128)(2,1)} %get-tuple-element.24.res_ref, bf16[16,64,128]{2,1,0:T(8,128)(2,1)} %get-tuple-element.17.rest_ref), custom_call_target="tpu_custom_call" | custom-call | tf_op jit(solution)/shard_map/combine/pallas_call | solution.py:643
  168.8 1.9 %copy.18 = bf16[256,1024]{1,0:T(8,128)(2,1)} copy(bf16[256,1024]{1,0:T(8,128)(2,1)} %combine.1) | data formatting | bytes 1048576
